TPU v7x, 32 devices: a whole 2x2x4 slice. The times are simulated.
32 devices in a mesh: req: 16 (over z, y, x), tp: 2 (over core).
Axes of the slice: x: 2, y: 2, z: 4, core: 2. Of those that a mesh axis runs over, the one named last changes fastest.
Arguments:
- hidden: bfloat16 [384, 4096], P('req', 'tp'), may hold values from -100 to 100
- norm_gain: float32 [4096], replicated, may hold values from 0.5 to 1.5
- norm_bias: float32 [4096], replicated, may hold values from -3 to 3
- unembed: bfloat16 [3136, 4096], P(('req', 'tp')), as said below
- targets: int32 [384], P('req'), may hold values from 0 to 3135
- span_start: int32 [48], P('req'), may hold values from 0 to 24, as said below
- span_end: int32 [48], P('req'), may hold values from 0 to 24, as said below
Outputs:
- logprob: float32 [384], P('req')
- entropy: float32 [384], P('req')
Inputs may be any that keep to these rules, and one draw needn't show every extreme that they name: A device's 3 spans are entries i * 3 to i * 3 + 2 of span_start and span_end; they are ordered and disjoint within its 24 rows, with start <= end (a span may be empty). Summed over all req devices, the rows inside spans number 12 times the number of req devices; a single device may hold from 1 to 24 of them, and on at least one device all 24 rows are inside spans. `span_end`: paired with span_start as stated there. `unembed`: entries lie within 20 / sqrt(4096) + 1600 / 4096 in magnitude.
All inputs are finite; a program needn't handle non-finite values.
Results may differ from a plain program's by a relative error of at most 0.0029.
Values may be sent and summed in bfloat16 or wider, within the bound.
No kernel may reach another device: no remote copies, remote signals or barrier semaphores. Data moves between devices by JAX's collectives and lax.ppermute only.
A program may use at most 64 MiB of HBM per device.

v0:
```python
import jax
import jax.numpy as jnp
from jax import lax
from jax.sharding import PartitionSpec as P

EPSILON = 1e-05


def live_mask(span_start, span_end, slot_count):
    position = jnp.arange(slot_count, dtype=jnp.int32)
    inside = (span_start[..., None] <= position) & (position < span_end[..., None])
    return jnp.any(inside, axis=-2)


def normalize(hidden, norm_gain, norm_bias):
    values = hidden.astype(jnp.float32)
    feature_count = values.shape[1]
    row_mean = jnp.sum(values, axis=1, keepdims=True) / feature_count
    row_square = jnp.sum(values * values, axis=1, keepdims=True) / feature_count
    scaled = (values - row_mean) * lax.rsqrt(row_square - row_mean * row_mean + EPSILON)
    return (scaled * norm_gain + norm_bias).astype(jnp.bfloat16)


def local(hidden, norm_gain, norm_bias, unembed, targets, span_start, span_end):
    slot_count = hidden.shape[0]
    tp_count = lax.axis_size("tp")
    req_rank = lax.axis_index("req")
    tp_rank = lax.axis_index("tp")
    vocab_part = unembed.shape[0]
    vocab_first = (req_rank * tp_count + tp_rank) * vocab_part
    live_mine = live_mask(span_start.reshape(1, -1), span_end.reshape(1, -1), slot_count).reshape(
        -1
    )
    row_ids = lax.all_gather(targets, "req", axis=0, tiled=True)
    full_rows = lax.all_gather(hidden, "tp", axis=1, tiled=True)
    normed = normalize(full_rows, norm_gain, norm_bias)
    scores = lax.dot_general(
        unembed,
        lax.all_gather(normed, "req", axis=0, tiled=True),
        (((1,), (1,)), ((), ())),
        preferred_element_type=jnp.float32,
    )
    vocab_ids = vocab_first + jnp.arange(vocab_part, dtype=jnp.int32)
    target_hit = jnp.sum(jnp.where(vocab_ids[:, None] == row_ids[None, :], scores, 0.0), axis=0)
    row_top = lax.pmax(jnp.max(scores, axis=0), ("req", "tp"))
    weights = jnp.exp(scores - row_top)
    row_total, row_spread, target_hit = lax.psum(
        (jnp.sum(weights, axis=0), jnp.sum(weights * (scores - row_top), axis=0), target_hit),
        ("req", "tp"),
    )
    log_total = jnp.log(row_total)
    logprob_all = target_hit - row_top - log_total
    entropy_all = log_total - row_spread / row_total
    logprob_mine = lax.dynamic_slice_in_dim(logprob_all, req_rank * slot_count, slot_count)
    entropy_mine = lax.dynamic_slice_in_dim(entropy_all, req_rank * slot_count, slot_count)
    return (jnp.where(live_mine, logprob_mine, 0.0), jnp.where(live_mine, entropy_mine, 0.0))


def solution(mesh):
    return jax.shard_map(
        local,
        mesh=mesh,
        in_specs=(P("req", "tp"), P(), P(), P(("req", "tp"), None), P("req"), P("req"), P("req")),
        out_specs=(P("req"), P("req")),
        check_vma=False,
    )
```

profile of v0, /device:TPU:0, one launch (start us, length us, event | category | flops | bytes accessed | tf_op | source)
XLA Modules:
  0.0 171.8 jit_solution(11994547703689368349)
XLA Ops:
  7.2 0.0 copy-start
  7.2 0.0 all-gather.2.cloned.1.call-start
  7.2 2.4 %all_gather.10 = bf16[24,4096]{1,0:T(8,128)(2,1)S(1)} all-gather(bf16[24,2048]{1,0:T(8,128)(2,1)} %param.7), channel_id=1, replica_groups=mesh['req'=16,'tp'=2] {'tp'}, dimensions={1}, use_global_device_ids=true | all-gather | bytes 294912 | tf_op jit(solution)/shard_map/all_gather | solution.py:35
  9.6 0.2 convert_reduce_fusion
  9.8 1.6 fusion.3
  11.4 0.0 all-gather.2.cloned.1.call-update
  11.4 1.2 dynamic-slice
  13.3 0.9 dynamic-update-slice
  14.2 16.2 %all-reduce = s32[384]{0:T(512)S(1)} all-reduce(s32[384]{0:T(512)S(1)} %dynamic-update-slice), channel_id=1, replica_groups=mesh['req'=16,'tp'=2] {'req'}, use_global_device_ids=true, to_apply=%add | all-reduce | flops 384 | bytes 3072
  30.4 0.8 fusion.8
  31.2 50.9 %all-gather.2.cloned.1.call-done = bf16[384,4096]{1,0:T(8,128)(2,1)} async-done(((bf16[24,4096]{1,0:T(8,128)(2,1)}), bf16[384,4096]{1,0:T(8,128)(2,1)}) %all-gather.2.cloned.1.call-update) | async-done | bytes 3145744 | tf_op jit(solution)/shard_map/all_gather | solution.py:39
  82.0 0.0 copy-done
  82.0 3.0 %fusion.9 = (f32[384]{0:T(512)S(1)}, f32[384,98]{0,1:T(8,128)S(1)}) fusion(bf16[384,4096]{1,0:T(8,128)(2,1)} %all-gather.2.cloned.1.call-done, bf16[98,4096]{1,0:T(8,128)(2,1)S(1)} %copy-done), kind=kOutput, calls=%fused_computation.25 | convolution fusion | flops 308318592 | bytes 4100608 | tf_op jit(solution)/shard_map/dot_general | solution.py:37
  85.0 39.2 %pmax.7 = f32[384]{0:T(512)S(1)} all-reduce(f32[384]{0:T(512)S(1)} %get-tuple-element.16), channel_id=1, replica_groups=mesh['req'=16,'tp'=2] {'req','tp'}, use_global_device_ids=true, to_apply=%region_6.7 | all-reduce | flops 384 | bytes 3072 | tf_op jit(solution)/shard_map/pmax | solution.py:45
  124.2 0.1 fusion.5
  124.3 40.0 %all-reduce.1 = (f32[384]{0:T(512)S(1)}, f32[384]{0:T(512)S(1)}, f32[384]{0:T(512)S(1)}) all-reduce(f32[384]{0:T(512)S(1)} %get-tuple-element.6, f32[384]{0:T(512)S(1)} %get-tuple-element.5, f32[384]{0:T(512)S(1)} %get-tuple-element.4), channel_id=1, replica_groups=mesh['req'=16,'tp'=2] {'req','tp'}, use_global_device_ids=true, to_apply=%region_4.5 | all-reduce | flops 1152 | bytes 9216 | tf_op jit(solution)/shard_map/psum | solution.py:47
  164.4 0.6 dynamic-slice_select_fusion
  (4 shorter events, 0.0 us)
Async XLA Ops:
  7.2 74.9 %copy-start = (bf16[98,4096]{1,0:T(8,128)(2,1)S(1)}, bf16[98,4096]{1,0:T(8,128)(2,1)}, u32[]{:S(2)}) copy-start(bf16[98,4096]{1,0:T(8,128)(2,1)} %param.10) | copy-start | bytes 2408452
  7.2 74.9 %all-gather.2.cloned.1.call-start = ((), (), s32[]{:S(2)}) async-start(), calls=%async_computation | async-start | bytes 3342336 | tf_op jit(solution)/shard_map/all_gather | solution.py:39
Sparse Core Ops, SparseCore 0:
  11.5 70.4 all-gather.1
where the time goes:
time: 172 us
  blocking collectives  97.9 us (57%)
  waiting for transfers between devices  50.9 us (30%)
  between operations  14.7 us (9%)
  other arithmetic  3.21 us (2%)
  matrix products  2.97 us (2%)
  local copies, waits for them, and re-layouts  2.11 us (1%)
    all_gather x1, waiting for transfers between devices, local(): lax.all_gather(normed, 'req', axis=0, tiled=True)  50.9 us
    psum x1, blocking collectives, local(): lax.psum((jnp.sum(weights, axis=0), jnp.sum(weights * (scores - row_top),...  40 us
    pmax x1, blocking collectives, local(): row_top = lax.pmax(jnp.max(scores, axis=0), ('req', 'tp'))  39.2 us
    unnamed x1, blocking collectives  16.2 us
  transfers between devices with their start and end apart: 1, of which 1 were waited for; matrix products, arithmetic and copies ran while one was open for 2% of the time, Pallas kernels for 0%

commit v1 on v0

--- a/solution.py
+++ b/solution.py
@@ -21,7 +21,7 @@
     return (scaled * norm_gain + norm_bias).astype(jnp.bfloat16)
 
 
-def local(hidden, norm_gain, norm_bias, unembed, targets, span_start, span_end):
+def gathered(hidden, norm_gain, norm_bias, unembed, targets, span_start, span_end):
     slot_count = hidden.shape[0]
     tp_count = lax.axis_size("tp")
     req_rank = lax.axis_index("req")
@@ -56,9 +56,115 @@
     return (jnp.where(live_mine, logprob_mine, 0.0), jnp.where(live_mine, entropy_mine, 0.0))
 
 
+X_BIT, Y_BIT, Z_NEAR, Z_FAR = 1, 2, 4, 8
+
+
+def exchange(value, bits):
+    pairs = [
+        (chip * 2 + core, (chip ^ bits[core]) * 2 + core) for chip in range(16) for core in range(2)
+    ]
+    return lax.ppermute(value, ("req", "tp"), pairs)
+
+
+def core_swap(value):
+    return lax.ppermute(value, "tp", [(0, 1), (1, 0)])
+
+
+ROW_STAGES = ((Z_FAR, Z_FAR), (X_BIT, Y_BIT), (Y_BIT, X_BIT))
+
+
+def block_partials(rows, row_ids, blocks, firsts):
+    scores = [
+        lax.dot_general(
+            block, rows, (((1,), (1,)), ((), ())), preferred_element_type=jnp.float32
+        )
+        for block in blocks
+    ]
+    top = jnp.max(scores[0], axis=0)
+    for part in scores[1:]:
+        top = jnp.maximum(top, jnp.max(part, axis=0))
+    total = jnp.zeros_like(top)
+    spread = jnp.zeros_like(top)
+    hit = jnp.zeros_like(top)
+    for part, first in zip(scores, firsts):
+        shifted = part - top
+        weights = jnp.exp(shifted)
+        total += jnp.sum(weights, axis=0)
+        spread += jnp.sum(weights * shifted, axis=0)
+        ids = first + jnp.arange(part.shape[0], dtype=jnp.int32)
+        hit += jnp.sum(jnp.where(ids[:, None] == row_ids[None, :], part, 0.0), axis=0)
+    return jnp.stack([top, total, spread, hit])
+
+
+def merge(one, two):
+    top = jnp.maximum(one[0], two[0])
+    down_one, down_two = one[0] - top, two[0] - top
+    scale_one, scale_two = jnp.exp(down_one), jnp.exp(down_two)
+    total = scale_one * one[1] + scale_two * two[1]
+    spread = scale_one * (one[2] + one[1] * down_one) + scale_two * (two[2] + two[1] * down_two)
+    return jnp.stack([top, total, spread, one[3] + two[3]])
+
+
+def paired(hidden, norm_gain, norm_bias, unembed, targets, span_start, span_end):
+    slot_count, feature_part = hidden.shape
+    half = slot_count // 2
+    width = 2 * feature_part
+    req_rank = lax.axis_index("req")
+    tp_rank = lax.axis_index("tp")
+    first_core = tp_rank == 0
+    vocab_part = unembed.shape[0]
+
+    other = core_swap(hidden)
+    near = exchange(unembed, (Z_NEAR, Z_NEAR))
+    blocks = [unembed, core_swap(unembed), near, core_swap(near)]
+    owners = [
+        (chip * 2 + core)
+        for chip in (req_rank, req_rank ^ Z_NEAR)
+        for core in (tp_rank, 1 - tp_rank)
+    ]
+    firsts = [owner * vocab_part for owner in owners]
+
+    def mine(value):
+        return jnp.where(first_core, value[:half], value[half:])
+
+    full_rows = jnp.where(
+        first_core,
+        jnp.concatenate([mine(hidden), mine(other)], axis=1),
+        jnp.concatenate([mine(other), mine(hidden)], axis=1),
+    )
+    normed = normalize(full_rows, norm_gain, norm_bias)
+    ids = mine(targets)
+    id_columns = jnp.stack([ids // 256, ids % 256], axis=1).astype(jnp.bfloat16)
+    rows = jnp.concatenate([normed, jnp.pad(id_columns, ((0, 0), (0, 126)))], axis=1)
+
+    def partials(part):
+        digits = part[:, width : width + 2].astype(jnp.int32)
+        return block_partials(part[:, :width], digits[:, 0] * 256 + digits[:, 1], blocks, firsts)
+
+    rows = jnp.concatenate([rows, exchange(rows, ROW_STAGES[0])], axis=0)
+    rows = jnp.concatenate([rows, exchange(rows, ROW_STAGES[1])], axis=0)
+    rows_far = exchange(rows, ROW_STAGES[2])
+    stats = merge(partials(rows), exchange(partials(rows_far), ROW_STAGES[2]))
+    for bits in ROW_STAGES[1::-1]:
+        keep = stats.shape[1] // 2
+        stats = merge(stats[:, :keep], exchange(stats[:, keep:], bits))
+    log_total = jnp.log(stats[1])
+    result = jnp.stack([stats[3] - stats[0] - log_total, log_total - stats[2] / stats[1]])
+    partner = core_swap(result)
+    both = jnp.where(
+        first_core,
+        jnp.concatenate([result, partner], axis=1),
+        jnp.concatenate([partner, result], axis=1),
+    )
+    live = live_mask(span_start, span_end, slot_count)
+    both = jnp.where(live, both, 0.0)
+    return both[0], both[1]
+
+
 def solution(mesh):
+    chips_of_two = mesh.shape["req"] == 16 and mesh.shape["tp"] == 2
     return jax.shard_map(
-        local,
+        paired if chips_of_two else gathered,
         mesh=mesh,
         in_specs=(P("req", "tp"), P(), P(), P(("req", "tp"), None), P("req"), P("req"), P("req")),
         out_specs=(P("req"), P("req")),

time: 172 us -> 57.8 us (0.34)
  blocking collectives: 97.9 us -> 0 us
  waiting for transfers between devices: 50.9 us -> 31.5 us
  starting transfers between devices: 0.04 us -> 15.8 us
  between operations: 14.7 us -> 0.85 us
    all_gather x1 -> x0, waiting for transfers between devices: 50.9 us -> none  [local(): lax.all_gather(normed, 'req', axis=0, tiled=True)]
    psum x1 -> x0, blocking collectives: 40 us -> none  [local(): lax.psum((jnp.sum(weights, axis=0), jnp.sum(weights * (scores - row_top),...]
    pmax x1 -> x0, blocking collectives: 39.2 us -> none  [local(): row_top = lax.pmax(jnp.max(scores, axis=0), ('req', 'tp'))]
    ppermute x0 -> x11, waiting for transfers between devices: none -> 31.5 us  [the longest x7 30.8 us: exchange(): return lax.ppermute(value, ('req', 'tp'), pairs)]
    unnamed x1 -> x0, blocking collectives: 16.2 us -> none
    ppermute x0 -> x11, starting transfers between devices: none -> 15.8 us  [the longest x7 14.9 us: exchange(): return lax.ppermute(value, ('req', 'tp'), pairs)]
    all_gather x1 -> x0, blocking collectives: 2.42 us -> none  [local(): full_rows = lax.all_gather(hidden, 'tp', axis=1, tiled=True)]
    dot_general x1 -> x8, matrix products: 2.97 us -> 4.23 us  [block_partials(): lax.dot_general(block, rows, (((1,), (1,)), ((), ())), preferred_element_...]
  transfers between devices with their start and end apart: 1 -> 11, of which waited for: 1 -> 8; matrix products, arithmetic and copies ran while one was open for 2% -> 10% of each run, Pallas kernels for 0% -> 0%
where the time goes in v1:
time: 57.8 us; the launch traced here: 57.1 us
  waiting for transfers between devices  31.5 us (54%)
  starting transfers between devices  15.8 us (27%)
  matrix products  4.23 us (7%)
  other arithmetic  2.95 us (5%)
  local copies, waits for them, and re-layouts  1.87 us (3%)
  between operations  0.85 us (1%)
    ppermute x7, waiting for transfers between devices, exchange(): return lax.ppermute(value, ('req', 'tp'), pairs)  30.8 us
    ppermute x7, starting transfers between devices, exchange(): return lax.ppermute(value, ('req', 'tp'), pairs)  14.9 us
    dot_general x8, matrix products, block_partials(): lax.dot_general(block, rows, (((1,), (1,)), ((), ())), preferred_element_...  4.23 us
    unnamed x13, local copies, waits for them, and re-layouts  1.19 us
  transfers between devices with their start and end apart: 11, of which 8 were waited for; matrix products, arithmetic and copies ran while one was open for 10% of the time, Pallas kernels for 0%

profile of v1, /device:TPU:0, one launch (start us, length us, event | category | flops | bytes accessed | tf_op | source)
XLA Modules:
  0.0 57.1 jit_solution(3478835605204344556)
XLA Ops:
  0.6 0.6 collective-permute-start.3
  1.2 2.6 %collective-permute-start.4 = (bf16[98,4096]{1,0:T(8,128)(2,1)}, bf16[98,4096]{1,0:T(8,128)(2,1)S(1)}, u32[]{:S(2)}, u32[]{:S(2)}) collective-permute-start(bf16[98,4096]{1,0:T(8,128)(2,1)} %param.10), channel_id=1, source_target_pairs={{0,8},{1,9},{2,10},{3,11},{4,12},{5,13},{6,14},{7,15},{8,0},{9,1},... | collective-permute-start | bytes 2408456 | tf_op jit(solution)/shard_map/ppermute | solution.py:66
  4.0 0.9 %slice_select_fusion.1 = bf16[12,2048]{1,0:T(8,128)(2,1)S(1)} fusion(bf16[24,2048]{1,0:T(8,128)(2,1)} %param.7, pred[]{:T(512)S(6)} %eq.32), kind=kLoop, calls=%fused_computation.29 | loop fusion | flops 24576 | bytes 147457 | tf_op jit(solution)/shard_map/jit(_where)/select_n | solution.py:128
  6.3 2.7 %collective-permute-start.1 = (bf16[12,4224]{1,0:T(8,128)(2,1)S(1)}, bf16[12,4224]{1,0:T(8,128)(2,1)S(1)}, u32[]{:S(2)}, u32[]{:S(2)}) collective-permute-start(bf16[12,4224]{1,0:T(8,128)(2,1)S(1)} %pad_maximum_fusion.2), channel_id=1, source_target_pairs={{0,16},{1,17},{2,18},{3,19},{4,20},{5,21},{6,22},{7,23},{8,24},{9,... | collective-permute-start | bytes 304136 | tf_op jit(solution)/shard_map/ppermute | solution.py:66
  8.9 16.8 %collective-permute-done.1 = bf16[12,4224]{1,0:T(8,128)(2,1)S(1)} collective-permute-done((bf16[12,4224]{1,0:T(8,128)(2,1)S(1)}, bf16[12,4224]{1,0:T(8,128)(2,1)S(1)}, u32[]{:S(2)}, u32[]{:S(2)}) %collective-permute-start.1) | collective-permute-done | bytes 101408 | tf_op jit(solution)/shard_map/ppermute | solution.py:66
  25.8 1.6 %collective-permute-start.2 = (bf16[24,4224]{1,0:T(8,128)(2,1)S(1)}, bf16[24,4224]{1,0:T(8,128)(2,1)S(1)}, u32[]{:S(2)}, u32[]{:S(2)}) collective-permute-start(bf16[24,4224]{1,0:T(8,128)(2,1)S(1)} %pad_maximum_fusion.1), channel_id=1, source_target_pairs={{0,2},{1,5},{2,0},{3,7},{4,6},{5,1},{6,4},{7,3},{8,10},{9,13},{10,... | collective-permute-start | bytes 608264 | tf_op jit(solution)/shard_map/ppermute | solution.py:66
  27.4 4.2 %collective-permute-done.2 = bf16[24,4224]{1,0:T(8,128)(2,1)S(1)} collective-permute-done((bf16[24,4224]{1,0:T(8,128)(2,1)S(1)}, bf16[24,4224]{1,0:T(8,128)(2,1)S(1)}, u32[]{:S(2)}, u32[]{:S(2)}) %collective-permute-start.2) | collective-permute-done | bytes 202784 | tf_op jit(solution)/shard_map/ppermute | solution.py:66
  31.7 1.6 %collective-permute-start.6 = (bf16[48,4224]{1,0:T(8,128)(2,1)S(1)}, bf16[48,4224]{1,0:T(8,128)(2,1)S(1)}, u32[]{:S(2)}, u32[]{:S(2)}) collective-permute-start(bf16[48,4224]{1,0:T(8,128)(2,1)S(1)} %pad_maximum_fusion), channel_id=1, source_target_pairs={{0,4},{1,3},{2,6},{3,1},{4,0},{5,7},{6,2},{7,5},{8,12},{9,11},{10,... | collective-permute-start | bytes 1216520 | tf_op jit(solution)/shard_map/ppermute | solution.py:66
  33.5 0.5 fusion.53
  34.1 0.5 fusion.52
  34.6 0.5 fusion.54
  35.1 4.5 %collective-permute-done.6 = bf16[48,4224]{1,0:T(8,128)(2,1)S(1)} collective-permute-done((bf16[48,4224]{1,0:T(8,128)(2,1)S(1)}, bf16[48,4224]{1,0:T(8,128)(2,1)S(1)}, u32[]{:S(2)}, u32[]{:S(2)}) %collective-permute-start.6) | collective-permute-done | bytes 405536 | tf_op jit(solution)/shard_map/ppermute | solution.py:66
  39.8 0.5 fusion.49
  40.4 0.5 fusion.50
  40.9 0.5 fusion.48
  41.4 0.5 fusion.47
  42.4 1.6 %collective-permute-start.7 = (f32[4,48]{1,0:T(4,128)S(1)}, f32[4,48]{1,0:T(4,128)S(1)}, u32[]{:S(2)}, u32[]{:S(2)}) collective-permute-start(f32[4,48]{1,0:T(4,128)S(1)} %pad_maximum_fusion.3), channel_id=1, source_target_pairs={{0,4},{1,3},{2,6},{3,1},{4,0},{5,7},{6,2},{7,5},{8,12},{9,11},{10,... | collective-permute-start | bytes 2312 | tf_op jit(solution)/shard_map/ppermute | solution.py:66
  44.0 0.5 fusion.51
  44.5 1.5 %collective-permute-done.7 = f32[4,48]{1,0:T(4,128)S(1)} collective-permute-done((f32[4,48]{1,0:T(4,128)S(1)}, f32[4,48]{1,0:T(4,128)S(1)}, u32[]{:S(2)}, u32[]{:S(2)}) %collective-permute-start.7) | collective-permute-done | bytes 800 | tf_op jit(solution)/shard_map/ppermute | solution.py:66
  46.5 1.5 %collective-permute-start.8 = (f32[4,24]{1,0:T(4,128)S(1)}, f32[4,24]{1,0:T(4,128)S(1)}, u32[]{:S(2)}, u32[]{:S(2)}) collective-permute-start(f32[4,24]{1,0:T(4,128)S(1)} %slice.165), channel_id=1, source_target_pairs={{0,2},{1,5},{2,0},{3,7},{4,6},{5,1},{6,4},{7,3},{8,10},{9,13},{10,... | collective-permute-start | bytes 1160 | tf_op jit(solution)/shard_map/ppermute | solution.py:66
  48.0 2.1 %collective-permute-done.8 = f32[4,24]{1,0:T(4,128)S(1)} collective-permute-done((f32[4,24]{1,0:T(4,128)S(1)}, f32[4,24]{1,0:T(4,128)S(1)}, u32[]{:S(2)}, u32[]{:S(2)}) %collective-permute-start.8) | collective-permute-done | bytes 416 | tf_op jit(solution)/shard_map/ppermute | solution.py:66
  50.3 3.4 %collective-permute-start.9 = (f32[4,12]{1,0:T(4,128)S(1)}, f32[4,12]{1,0:T(4,128)S(1)}, u32[]{:S(2)}, u32[]{:S(2)}) collective-permute-start(f32[4,12]{1,0:T(4,128)S(1)} %slice.174), channel_id=1, source_target_pairs={{0,16},{1,17},{2,18},{3,19},{4,20},{5,21},{6,22},{7,23},{8,24},{9,... | collective-permute-start | bytes 584 | tf_op jit(solution)/shard_map/ppermute | solution.py:66
  53.6 1.6 %collective-permute-done.9 = f32[4,12]{1,0:T(4,128)S(1)} collective-permute-done((f32[4,12]{1,0:T(4,128)S(1)}, f32[4,12]{1,0:T(4,128)S(1)}, u32[]{:S(2)}, u32[]{:S(2)}) %collective-permute-start.9) | collective-permute-done | bytes 224 | tf_op jit(solution)/shard_map/ppermute | solution.py:66
  55.4 0.5 copy-done.4
  (60 shorter events, 4.3 us)
Async XLA Ops:
  0.6 34.0 %collective-permute-start.3 = (bf16[98,4096]{1,0:T(8,128)(2,1)}, bf16[98,4096]{1,0:T(8,128)(2,1)S(1)}, u32[]{:S(2)}, u32[]{:S(2)}) collective-permute-start(bf16[98,4096]{1,0:T(8,128)(2,1)} %param.10), channel_id=1, source_target_pairs={{0,1},{1,0},{2,3},{3,2},{4,5},{5,4},{6,7},{7,6},{8,9},{9,8},{10,11... | collective-permute-start | bytes 2408456 | tf_op jit(solution)/shard_map/ppermute | solution.py:70
  1.2 32.8 %collective-permute-start.4 = (bf16[98,4096]{1,0:T(8,128)(2,1)}, bf16[98,4096]{1,0:T(8,128)(2,1)S(1)}, u32[]{:S(2)}, u32[]{:S(2)}) collective-permute-start(bf16[98,4096]{1,0:T(8,128)(2,1)} %param.10), channel_id=1, source_target_pairs={{0,8},{1,9},{2,10},{3,11},{4,12},{5,13},{6,14},{7,15},{8,0},{9,1},... | collective-permute-start | bytes 2408456 | tf_op jit(solution)/shard_map/ppermute | solution.py:66
  3.8 1.5 %collective-permute-start = (bf16[24,2048]{1,0:T(8,128)(2,1)}, bf16[24,2048]{1,0:T(8,128)(2,1)S(1)}, u32[]{:S(2)}, u32[]{:S(2)}) collective-permute-start(bf16[24,2048]{1,0:T(8,128)(2,1)} %param.7), channel_id=1, source_target_pairs={{0,1},{1,0},{2,3},{3,2},{4,5},{5,4},{6,7},{7,6},{8,9},{9,8},{10,11... | collective-permute-start | bytes 294920 | tf_op jit(solution)/shard_map/ppermute | solution.py:70
  4.0 0.9 %copy-start.3 = (s32[24]{0:T(128)S(1)}, s32[24]{0:T(128)}, u32[]{:S(2)}) copy-start(s32[24]{0:T(128)} %param.11) | copy-start | bytes 292
  5.4 0.7 %copy-start.1 = (f32[4096]{0:T(1024)S(1)}, f32[4096]{0:T(1024)}, u32[]{:S(2)}) copy-start(f32[4096]{0:T(1024)} %param.9) | copy-start | bytes 49156
  5.4 0.7 %copy-start.2 = (f32[4096]{0:T(1024)S(1)}, f32[4096]{0:T(1024)}, u32[]{:S(2)}) copy-start(f32[4096]{0:T(1024)} %param.8) | copy-start | bytes 49156
  6.2 27.2 %copy-start = (bf16[98,4096]{1,0:T(8,128)(2,1)S(1)}, bf16[98,4096]{1,0:T(8,128)(2,1)}, u32[]{:S(2)}) copy-start(bf16[98,4096]{1,0:T(8,128)(2,1)} %param.10) | copy-start | bytes 2408452
  6.3 19.5 %collective-permute-start.1 = (bf16[12,4224]{1,0:T(8,128)(2,1)S(1)}, bf16[12,4224]{1,0:T(8,128)(2,1)S(1)}, u32[]{:S(2)}, u32[]{:S(2)}) collective-permute-start(bf16[12,4224]{1,0:T(8,128)(2,1)S(1)} %pad_maximum_fusion.2), channel_id=1, source_target_pairs={{0,16},{1,17},{2,18},{3,19},{4,20},{5,21},{6,22},{7,23},{8,24},{9,... | collective-permute-start | bytes 304136 | tf_op jit(solution)/shard_map/ppermute | solution.py:66
  25.8 5.8 %collective-permute-start.2 = (bf16[24,4224]{1,0:T(8,128)(2,1)S(1)}, bf16[24,4224]{1,0:T(8,128)(2,1)S(1)}, u32[]{:S(2)}, u32[]{:S(2)}) collective-permute-start(bf16[24,4224]{1,0:T(8,128)(2,1)S(1)} %pad_maximum_fusion.1), channel_id=1, source_target_pairs={{0,2},{1,5},{2,0},{3,7},{4,6},{5,1},{6,4},{7,3},{8,10},{9,13},{10,... | collective-permute-start | bytes 608264 | tf_op jit(solution)/shard_map/ppermute | solution.py:66
  31.7 8.0 %collective-permute-start.6 = (bf16[48,4224]{1,0:T(8,128)(2,1)S(1)}, bf16[48,4224]{1,0:T(8,128)(2,1)S(1)}, u32[]{:S(2)}, u32[]{:S(2)}) collective-permute-start(bf16[48,4224]{1,0:T(8,128)(2,1)S(1)} %pad_maximum_fusion), channel_id=1, source_target_pairs={{0,4},{1,3},{2,6},{3,1},{4,0},{5,7},{6,2},{7,5},{8,12},{9,11},{10,... | collective-permute-start | bytes 1216520 | tf_op jit(solution)/shard_map/ppermute | solution.py:66
  34.0 7.4 %collective-permute-start.5 = (bf16[98,4096]{1,0:T(8,128)(2,1)S(1)}, bf16[98,4096]{1,0:T(8,128)(2,1)S(1)}, u32[]{:S(2)}, u32[]{:S(2)}) collective-permute-start(bf16[98,4096]{1,0:T(8,128)(2,1)S(1)} %collective-permute-done.4), channel_id=1, source_target_pairs={{0,1},{1,0},{2,3},{3,2},{4,5},{5,4},{6,7},{7,6},{8,9},{9,8},{10,11... | collective-permute-start | bytes 2408456 | tf_op jit(solution)/shard_map/ppermute | solution.py:70
  42.4 3.7 %collective-permute-start.7 = (f32[4,48]{1,0:T(4,128)S(1)}, f32[4,48]{1,0:T(4,128)S(1)}, u32[]{:S(2)}, u32[]{:S(2)}) collective-permute-start(f32[4,48]{1,0:T(4,128)S(1)} %pad_maximum_fusion.3), channel_id=1, source_target_pairs={{0,4},{1,3},{2,6},{3,1},{4,0},{5,7},{6,2},{7,5},{8,12},{9,11},{10,... | collective-permute-start | bytes 2312 | tf_op jit(solution)/shard_map/ppermute | solution.py:66
  46.5 3.6 %collective-permute-start.8 = (f32[4,24]{1,0:T(4,128)S(1)}, f32[4,24]{1,0:T(4,128)S(1)}, u32[]{:S(2)}, u32[]{:S(2)}) collective-permute-start(f32[4,24]{1,0:T(4,128)S(1)} %slice.165), channel_id=1, source_target_pairs={{0,2},{1,5},{2,0},{3,7},{4,6},{5,1},{6,4},{7,3},{8,10},{9,13},{10,... | collective-permute-start | bytes 1160 | tf_op jit(solution)/shard_map/ppermute | solution.py:66
  50.3 5.0 %collective-permute-start.9 = (f32[4,12]{1,0:T(4,128)S(1)}, f32[4,12]{1,0:T(4,128)S(1)}, u32[]{:S(2)}, u32[]{:S(2)}) collective-permute-start(f32[4,12]{1,0:T(4,128)S(1)} %slice.174), channel_id=1, source_target_pairs={{0,16},{1,17},{2,18},{3,19},{4,20},{5,21},{6,22},{7,23},{8,24},{9,... | collective-permute-start | bytes 584 | tf_op jit(solution)/shard_map/ppermute | solution.py:66
  55.2 0.7 %copy-start.4 = (s32[3]{0:T(128)S(1)}, s32[3]{0:T(128)}, u32[]{:S(2)}) copy-start(s32[3]{0:T(128)} %param.13) | copy-start | bytes 40
  55.3 0.7 %copy-start.5 = (s32[3]{0:T(128)S(1)}, s32[3]{0:T(128)}, u32[]{:S(2)}) copy-start(s32[3]{0:T(128)} %param.12) | copy-start | bytes 40
  55.3 1.2 %collective-permute-start.10 = (f32[2,12]{1,0:T(2,128)S(1)}, f32[2,12]{1,0:T(2,128)S(1)}, u32[]{:S(2)}, u32[]{:S(2)}) collective-permute-start(f32[2,12]{1,0:T(2,128)S(1)} %pad_maximum_fusion.6), channel_id=1, source_target_pairs={{0,1},{1,0},{2,3},{3,2},{4,5},{5,4},{6,7},{7,6},{8,9},{9,8},{10,11... | collective-permute-start | bytes 296 | tf_op jit(solution)/shard_map/ppermute | solution.py:70

commit v2 on v0

--- a/solution.py
+++ b/solution.py
@@ -1,6 +1,10 @@
+import functools
+
 import jax
 import jax.numpy as jnp
 from jax import lax
+from jax.experimental import pallas as pl
+from jax.experimental.pallas import tpu as pltpu
 from jax.sharding import PartitionSpec as P
 
 EPSILON = 1e-05
@@ -21,7 +25,7 @@
     return (scaled * norm_gain + norm_bias).astype(jnp.bfloat16)
 
 
-def local(hidden, norm_gain, norm_bias, unembed, targets, span_start, span_end):
+def gathered(hidden, norm_gain, norm_bias, unembed, targets, span_start, span_end):
     slot_count = hidden.shape[0]
     tp_count = lax.axis_size("tp")
     req_rank = lax.axis_index("req")
@@ -56,9 +60,287 @@
     return (jnp.where(live_mine, logprob_mine, 0.0), jnp.where(live_mine, entropy_mine, 0.0))
 
 
+X_BIT, Y_BIT, Z_NEAR, Z_FAR = 1, 2, 4, 8
+FAR, FIRST, SECOND = (Z_FAR, Z_FAR), (X_BIT, Y_BIT), (Y_BIT, X_BIT)
+LANES = 128
+KERNEL_VMEM = 16 << 20
+CHUNKS = (24, 40)
+
+
+def exchange(value, bits):
+    pairs = [
+        (chip * 2 + core, (chip ^ bits[core]) * 2 + core) for chip in range(16) for core in range(2)
+    ]
+    return lax.ppermute(value, ("req", "tp"), pairs)
+
+
+def core_swap(value):
+    return lax.ppermute(value, "tp", [(0, 1), (1, 0)])
+
+
+def in_vmem(value):
+    return pltpu.with_memory_space_constraint(value, pltpu.VMEM)
+
+
+def my_half(ref, half):
+    value = ref[...].astype(jnp.float32)
+    return jnp.where(lax.axis_index("tp") == 0, value[:half], value[half:])
+
+
+def stage_kernel(cuts, half, hidden_in, gain_in, bias_in, unembed_in, ids_in, *refs):
+    hidden_ref, gain_ref, bias_ref, digit_ref, *chunks = refs[:-2]
+    ids_ref, sems = refs[-2:]
+    pairs = [(ids_in, ids_ref), (hidden_in, hidden_ref), (gain_in, gain_ref), (bias_in, bias_ref)]
+    pairs += [
+        (unembed_in.at[pl.ds(start, chunk.shape[0]), :], chunk)
+        for chunk, start in zip(chunks, cuts)
+    ]
+    copies = [pltpu.make_async_copy(*pair, sems.at[k]) for k, pair in enumerate(pairs)]
+    for copy in copies:
+        copy.start()
+    copies[0].wait()
+    core = lax.axis_index("tp")
+    row = lax.broadcasted_iota(jnp.int32, (half, LANES), 0)
+    lane = lax.broadcasted_iota(jnp.int32, (half, LANES), 1)
+    digits = jnp.zeros((half, LANES), jnp.int32)
+    for index in range(half):
+        row_id = ids_ref[core * half + index]
+        digit = jnp.where(lane == 0, row_id >> 8, jnp.where(lane == 1, row_id & 255, 0))
+        digits = jnp.where(row == index, digit, digits)
+    digit_ref[...] = digits.astype(jnp.float32).astype(jnp.bfloat16)
+    for copy in copies[1:]:
+        copy.wait()
+
+
+def in_hbm(value):
+    return pltpu.with_memory_space_constraint(value, pltpu.HBM)
+
+
+def stage(hidden, norm_gain, norm_bias, unembed, targets, cuts):
+    half = hidden.shape[0] // 2
+    width = norm_gain.shape[0]
+    vmem = pl.BlockSpec(memory_space=pltpu.VMEM)
+    chunks = [
+        pltpu.VMEM((stop - start, width), jnp.bfloat16) for start, stop in zip(cuts, cuts[1:])
+    ]
+    return pl.pallas_call(
+        functools.partial(stage_kernel, cuts, half),
+        out_shape=[
+            pltpu.VMEM(hidden.shape, hidden.dtype),
+            pltpu.VMEM((1, width), jnp.float32),
+            pltpu.VMEM((1, width), jnp.float32),
+            pltpu.VMEM((half, LANES), jnp.bfloat16),
+            *chunks,
+        ],
+        in_specs=[pl.BlockSpec(memory_space=pltpu.HBM)] * 5,
+        out_specs=[vmem] * (4 + len(chunks)),
+        scratch_shapes=[
+            pltpu.SMEM(targets.shape, jnp.int32),
+            pltpu.SemaphoreType.DMA((4 + len(chunks),)),
+        ],
+        compiler_params=pltpu.CompilerParams(vmem_limit_bytes=KERNEL_VMEM),
+        name="stage",
+    )(
+        *map(
+            in_hbm, (hidden, norm_gain.reshape(1, -1), norm_bias.reshape(1, -1), unembed, targets)
+        )
+    )
+
+
+def normalize_kernel(own_ref, other_ref, gain_ref, bias_ref, digit_ref, rows_ref):
+    half, part = rows_ref.shape[0], own_ref.shape[1]
+    first_core = lax.axis_index("tp") == 0
+    own, other = my_half(own_ref, half), my_half(other_ref, half)
+    low, high = jnp.where(first_core, own, other), jnp.where(first_core, other, own)
+    sides = ((low, 0), (high, part))
+    row_mean = sum(jnp.sum(side, axis=1, keepdims=True) for side, _ in sides) / (2 * part)
+    row_square = sum(jnp.sum(side * side, axis=1, keepdims=True) for side, _ in sides) / (2 * part)
+    scale = lax.rsqrt(row_square - row_mean * row_mean + EPSILON)
+    for side, start in sides:
+        columns = pl.ds(start, part)
+        scaled = (side - row_mean) * scale
+        rows_ref[:, columns] = (scaled * gain_ref[:, columns] + bias_ref[:, columns]).astype(
+            jnp.bfloat16
+        )
+    rows_ref[:, pl.ds(2 * part, LANES)] = digit_ref[...]
+
+
+def normalize_rows(own, other, gain, bias, digits):
+    half, part = own.shape[0] // 2, own.shape[1]
+    vmem = pl.BlockSpec(memory_space=pltpu.VMEM)
+    return pl.pallas_call(
+        normalize_kernel,
+        out_shape=pltpu.VMEM((half, 2 * part + LANES), jnp.bfloat16),
+        in_specs=[vmem] * 5,
+        out_specs=vmem,
+        compiler_params=pltpu.CompilerParams(vmem_limit_bytes=KERNEL_VMEM),
+        name="normalize_rows",
+    )(*map(in_vmem, (own, other, gain, bias, digits)))
+
+
+def merge(one, two):
+    top = jnp.maximum(one[0], two[0])
+    down_one, down_two = one[0] - top, two[0] - top
+    scale_one, scale_two = jnp.exp(down_one), jnp.exp(down_two)
+    total = scale_one * one[1] + scale_two * two[1]
+    spread = scale_one * (one[2] + one[1] * down_one) + scale_two * (two[2] + two[1] * down_two)
+    return top, total, spread, one[3] + two[3]
+
+
+def partials_kernel(places, vocab_part, pieces, *refs):
+    count = len(places)
+    piece_refs, blocks = refs[:pieces], refs[pieces : pieces + count]
+    earlier, outs, rows_ref = refs[pieces + count : -3], refs[-3:-1], refs[-1]
+    width = blocks[0].shape[1]
+    row_count = rows_ref.shape[0]
+    piece_rows = row_count // pieces
+    for index, piece in enumerate(piece_refs):
+        rows_ref[pl.ds(index * piece_rows, piece_rows), :] = piece[...]
+    chip, core = lax.axis_index("req"), lax.axis_index("tp")
+
+    lane = lax.broadcasted_iota(jnp.int32, (16, LANES), 1)
+    pick = jnp.where(lane == 0, 256.0, jnp.where(lane == 1, 1.0, 0.0)).astype(jnp.bfloat16)
+    contract = (((1,), (1,)), ((), ()))
+    row_ids = lax.dot_general(
+        pick, rows_ref[:, pl.ds(width, LANES)], contract, preferred_element_type=jnp.float32
+    )[:1].astype(jnp.int32)
+    rows = rows_ref[:, pl.ds(0, width)]
+    scores = [
+        lax.dot_general(block[...], rows, contract, preferred_element_type=jnp.float32)
+        for block in blocks
+    ]
+    top = scores[0].max(axis=0, keepdims=True)
+    for part in scores[1:]:
+        top = jnp.maximum(top, part.max(axis=0, keepdims=True))
+    total = jnp.zeros((1, row_count), jnp.float32)
+    spread, hit = total, total
+    for part, (chip_bit, core_bit, start) in zip(scores, places):
+        shifted = part - top
+        weights = jnp.exp(shifted)
+        total += weights.sum(axis=0, keepdims=True)
+        spread += (weights * shifted).sum(axis=0, keepdims=True)
+        first = ((chip ^ chip_bit) * 2 + (core ^ core_bit)) * vocab_part + start
+        ids = first + lax.broadcasted_iota(jnp.int32, (part.shape[0], 1), 0)
+        hit += jnp.where(ids == row_ids, part, 0.0).sum(axis=0, keepdims=True)
+    stats = (top, total, spread, hit)
+    half = row_count // 2
+    if earlier:
+        before = [
+            jnp.concatenate([ref[pl.ds(k, 1), :] for ref in earlier], axis=1) for k in range(4)
+        ]
+        stats = merge(before, stats)
+    for k in range(4):
+        outs[0][pl.ds(k, 1), :] = stats[k][:, :half]
+        outs[1][pl.ds(k, 1), :] = stats[k][:, half:]
+
+
+def partials(rows, blocks, places, vocab_part, earlier=()):
+    row_count = len(rows) * rows[0].shape[0]
+    half = row_count // 2
+    vmem = pl.BlockSpec(memory_space=pltpu.VMEM)
+    return pl.pallas_call(
+        functools.partial(partials_kernel, places, vocab_part, len(rows)),
+        out_shape=[pltpu.VMEM((4, half), jnp.float32)] * 2,
+        in_specs=[vmem] * (len(rows) + len(blocks) + len(earlier)),
+        out_specs=[vmem] * 2,
+        scratch_shapes=[pltpu.VMEM((row_count, rows[0].shape[1]), jnp.bfloat16)],
+        compiler_params=pltpu.CompilerParams(vmem_limit_bytes=KERNEL_VMEM),
+        name="partials",
+    )(*map(in_vmem, (*rows, *blocks, *earlier)))
+
+
+def merge_kernel(group, mine_ref, theirs_ref, keep_ref, give_ref):
+    mine, theirs = ([ref[pl.ds(k, 1), :] for k in range(4)] for ref in (mine_ref, theirs_ref))
+    for k, value in enumerate(merge(mine, theirs)):
+        pieces = [value[:, at : at + group] for at in range(0, value.shape[1], group)]
+        keep_ref[pl.ds(k, 1), :] = jnp.concatenate(pieces[0::2], axis=1)
+        give_ref[pl.ds(k, 1), :] = jnp.concatenate(pieces[1::2], axis=1)
+
+
+def finish_kernel(mine_ref, theirs_ref, out_ref):
+    mine, theirs = ([ref[pl.ds(k, 1), :] for k in range(4)] for ref in (mine_ref, theirs_ref))
+    row_top, row_total, row_spread, target_hit = merge(mine, theirs)
+    log_total = jnp.log(row_total)
+    out_ref[pl.ds(0, 1), :] = target_hit - row_top - log_total
+    out_ref[pl.ds(1, 1), :] = log_total - row_spread / row_total
+
+
+def merge_and_split(mine, theirs, group):
+    vmem = pl.BlockSpec(memory_space=pltpu.VMEM)
+    return pl.pallas_call(
+        functools.partial(merge_kernel, group),
+        out_shape=[pltpu.VMEM((4, mine.shape[1] // 2), jnp.float32)] * 2,
+        in_specs=[vmem] * 2,
+        out_specs=[vmem] * 2,
+        compiler_params=pltpu.CompilerParams(vmem_limit_bytes=KERNEL_VMEM),
+        name="merge_and_split",
+    )(in_vmem(mine), in_vmem(theirs))
+
+
+def finish(mine, theirs):
+    vmem = pl.BlockSpec(memory_space=pltpu.VMEM)
+    return pl.pallas_call(
+        finish_kernel,
+        out_shape=pltpu.VMEM((2, mine.shape[1]), jnp.float32),
+        in_specs=[vmem] * 2,
+        out_specs=vmem,
+        compiler_params=pltpu.CompilerParams(vmem_limit_bytes=KERNEL_VMEM),
+        name="finish",
+    )(in_vmem(mine), in_vmem(theirs))
+
+
+def paired(hidden, norm_gain, norm_bias, unembed, targets, span_start, span_end):
+    slot_count = hidden.shape[0]
+    half = slot_count // 2
+    vocab_part = unembed.shape[0]
+    first_core = lax.axis_index("tp") == 0
+
+    cuts = [0, *[sum(CHUNKS[: k + 1]) for k in range(len(CHUNKS))], vocab_part]
+    other = core_swap(hidden)
+    own_part, gain, bias, digits, *chunks = stage(
+        hidden, norm_gain, norm_bias, unembed, targets, cuts
+    )
+    own = normalize_rows(own_part, other, gain, bias, digits)
+    near = [exchange(chunk, (Z_NEAR, Z_NEAR)) for chunk in chunks]
+    far = exchange(own, FAR)
+    own_side = exchange(own, FIRST)
+    far, own_side, near[0] = lax.optimization_barrier((far, own_side, near[0]))
+    near_rows = jnp.concatenate([own, own_side], axis=0)
+    near_across = exchange(near_rows, SECOND)
+    far_side = exchange(far, FIRST)
+    far_side, near_across, near[1] = lax.optimization_barrier((far_side, near_across, near[1]))
+    far_rows = jnp.concatenate([far, far_side], axis=0)
+    far_across = exchange(far_rows, SECOND)
+
+    blocks, places = [unembed, core_swap(unembed)], [(0, 0, 0), (0, 1, 0)]
+    for block, start in zip(near, cuts):
+        if start != cuts[-2]:
+            blocks += [block, core_swap(block)]
+            places += [(Z_NEAR, 0, start), (Z_NEAR, 1, start)]
+    rows = [near_rows, far_rows, near_across, far_across]
+    early = partials(rows, blocks, places, vocab_part)
+    last, early = lax.optimization_barrier((near[-1], early))
+    blocks = [last, core_swap(last)]
+    places = [(Z_NEAR, core_bit, cuts[-2]) for core_bit in (0, 1)]
+    keep, give = partials(rows, blocks, places, vocab_part, early)
+    keep, give = merge_and_split(keep, exchange(give, SECOND), half)
+    keep, give = merge_and_split(keep, exchange(give, FIRST), half)
+    result = finish(keep, exchange(give, FAR))
+    partner = core_swap(result)
+    both = jnp.where(
+        first_core,
+        jnp.concatenate([result, partner], axis=1),
+        jnp.concatenate([partner, result], axis=1),
+    )
+    live = live_mask(span_start, span_end, slot_count)
+    both = jnp.where(live, both, 0.0)
+    return both[0], both[1]
+
+
 def solution(mesh):
+    chips_of_two = mesh.shape["req"] == 16 and mesh.shape["tp"] == 2
     return jax.shard_map(
-        local,
+        paired if chips_of_two else gathered,
         mesh=mesh,
         in_specs=(P("req", "tp"), P(), P(), P(("req", "tp"), None), P("req"), P("req"), P("req")),
         out_specs=(P("req"), P("req")),

time: 172 us -> 45 us (0.26)
  blocking collectives: 97.9 us -> 0 us
  waiting for transfers between devices: 50.9 us -> 16.6 us
  starting transfers between devices: 0.04 us -> 22.4 us
  between operations: 14.7 us -> 0.72 us
  Pallas kernels: 0 us -> 4.34 us
  matrix products: 2.97 us -> 0 us
  other arithmetic: 3.21 us -> 0.28 us
    all_gather x1 -> x0, waiting for transfers between devices: 50.9 us -> none  [local(): lax.all_gather(normed, 'req', axis=0, tiled=True)]
    psum x1 -> x0, blocking collectives: 40 us -> none  [local(): lax.psum((jnp.sum(weights, axis=0), jnp.sum(weights * (scores - row_top),...]
    pmax x1 -> x0, blocking collectives: 39.2 us -> none  [local(): row_top = lax.pmax(jnp.max(scores, axis=0), ('req', 'tp'))]
    ppermute x0 -> x17, starting transfers between devices: none -> 22.4 us  [the longest x11 21.6 us: exchange(): return lax.ppermute(value, ('req', 'tp'), pairs)]
    ppermute x0 -> x17, waiting for transfers between devices: none -> 16.6 us  [the longest x11 12.5 us: exchange(): return lax.ppermute(value, ('req', 'tp'), pairs)]
    unnamed x1 -> x0, blocking collectives: 16.2 us -> none
    pallas_call x0 -> x7, Pallas kernels: none -> 4.34 us  [the longest x2 2.58 us: partials(): pl.pallas_call(functools.partial(partials_kernel, places, vocab_part, len...]
    dot_general x1 -> x0, matrix products: 2.97 us -> none  [local(): lax.dot_general(unembed, lax.all_gather(normed, 'req', axis=0, tiled=True...]
  transfers between devices with their start and end apart: 1 -> 17, of which waited for: 1 -> 9; matrix products, arithmetic and copies ran while one was open for 2% -> 0% of each run, Pallas kernels for 0% -> 8%
where the time goes in v2:
time: 45 us; the launch traced here: 44.9 us
  starting transfers between devices  22.4 us (50%)
  waiting for transfers between devices  16.6 us (37%)
  Pallas kernels  4.34 us (10%)
  between operations  0.72 us (2%)
  local copies, waits for them, and re-layouts  0.54 us (1%)
    ppermute x11, starting transfers between devices, exchange(): return lax.ppermute(value, ('req', 'tp'), pairs)  21.6 us
    ppermute x11, waiting for transfers between devices, exchange(): return lax.ppermute(value, ('req', 'tp'), pairs)  12.5 us
    ppermute x6, waiting for transfers between devices, core_swap(): return lax.ppermute(value, 'tp', [(0, 1), (1, 0)])  4.07 us
    pallas_call x2, Pallas kernels, partials(): pl.pallas_call(functools.partial(partials_kernel, places, vocab_part, len...  2.58 us
    pallas_call x1, Pallas kernels, stage(): pl.pallas_call(functools.partial(stage_kernel, cuts, half), out_shape=[pl...  1.38 us
  transfers between devices with their start and end apart: 17, of which 9 were waited for; matrix products, arithmetic and copies ran while one was open for 0% of the time, Pallas kernels for 8%

profile of v2, /device:TPU:0, one launch (start us, length us, event | category | flops | bytes accessed | tf_op | source)
XLA Modules:
  0.0 44.9 jit_solution(5346831304340246102)
XLA Ops:
  0.6 0.6 %collective-permute-start = (bf16[24,2048]{1,0:T(8,128)(2,1)}, bf16[24,2048]{1,0:T(8,128)(2,1)S(1)}, u32[]{:S(2)}, u32[]{:S(2)}) collective-permute-start(bf16[24,2048]{1,0:T(8,128)(2,1)} %hidden_in.1), channel_id=1, source_target_pairs={{0,1},{1,0},{2,3},{3,2},{4,5},{5,4},{6,7},{7,6},{8,9},{9,8},{10,11... | collective-permute-start | bytes 294920 | tf_op jit(solution)/shard_map/ppermute | solution.py:78
  1.2 1.4 %stage.1 = (bf16[24,2048]{1,0:T(8,128)(2,1)S(1)}, f32[1,4096]{1,0:T(1,128)S(1)}, f32[1,4096]{1,0:T(1,128)S(1)}, bf16[12,128]{1,0:T(8,128)(2,1)S(1)}, bf16[24,409...) custom-call(bf16[24,2048]{1,0:T(8,128)(2,1)} %hidden_in.1, f32[1,4096]{1,0:T(1,128)} %bitcast.6, ...), custom_call_target="tpu_custom_call" | custom-call | tf_op jit(solution)/shard_map/stage/pallas_call | solution.py:126
  2.6 2.6 %collective-permute-start.3 = (bf16[24,4096]{1,0:T(8,128)(2,1)S(1)}, bf16[24,4096]{1,0:T(8,128)(2,1)S(1)}, u32[]{:S(2)}, u32[]{:S(2)}) collective-permute-start(bf16[24,4096]{1,0:T(8,128)(2,1)S(1)} %get-tuple-element.30), channel_id=1, source_target_pairs={{0,8},{1,9},{2,10},{3,11},{4,12},{5,13},{6,14},{7,15},{8,0},{9,1},... | collective-permute-start | bytes 589832 | tf_op jit(solution)/shard_map/ppermute | solution.py:74
  5.4 2.7 %collective-permute-start.1 = (bf16[12,4224]{1,0:T(8,128)(2,1)S(1)}, bf16[12,4224]{1,0:T(8,128)(2,1)S(1)}, u32[]{:S(2)}, u32[]{:S(2)}) collective-permute-start(bf16[12,4224]{1,0:T(8,128)(2,1)S(1)} %normalize_rows.1), channel_id=1, source_target_pairs={{0,16},{1,17},{2,18},{3,19},{4,20},{5,21},{6,22},{7,23},{8,24},{9,... | collective-permute-start | bytes 304136 | tf_op jit(solution)/shard_map/ppermute | solution.py:74
  8.1 1.5 %collective-permute-start.2 = (bf16[12,4224]{1,0:T(8,128)(2,1)S(1)}, bf16[12,4224]{1,0:T(8,128)(2,1)S(1)}, u32[]{:S(2)}, u32[]{:S(2)}) collective-permute-start(bf16[12,4224]{1,0:T(8,128)(2,1)S(1)} %normalize_rows.1), channel_id=1, source_target_pairs={{0,2},{1,5},{2,0},{3,7},{4,6},{5,1},{6,4},{7,3},{8,10},{9,13},{10,... | collective-permute-start | bytes 304136 | tf_op jit(solution)/shard_map/ppermute | solution.py:74
  10.0 3.8 %collective-permute-done.3.refs_6_ = bf16[24,4096]{1,0:T(8,128)(2,1)S(1)} collective-permute-done((bf16[24,4096]{1,0:T(8,128)(2,1)S(1)}, bf16[24,4096]{1,0:T(8,128)(2,1)S(1)}, u32[]{:S(2)}, u32[]{:S(2)}) %collective-permute-start.3) | collective-permute-done | bytes 196640 | tf_op jit(solution)/shard_map/ppermute | solution.py:74
  13.9 2.0 %collective-permute-start.5 = (bf16[24,4224]{1,0:T(8,128)(2,1)S(1)}, bf16[24,4224]{1,0:T(8,128)(2,1)S(1)}, u32[]{:S(2)}, u32[]{:S(2)}) collective-permute-start(bf16[24,4224]{1,0:T(8,128)(2,1)S(1)} %pad_maximum_fusion.refs_0_), channel_id=1, source_target_pairs={{0,4},{1,3},{2,6},{3,1},{4,0},{5,7},{6,2},{7,5},{8,12},{9,11},{10,... | collective-permute-start | bytes 608264 | tf_op jit(solution)/shard_map/ppermute | solution.py:74
  16.0 1.5 %collective-permute-start.4 = (bf16[12,4224]{1,0:T(8,128)(2,1)S(1)}, bf16[12,4224]{1,0:T(8,128)(2,1)S(1)}, u32[]{:S(2)}, u32[]{:S(2)}) collective-permute-start(bf16[12,4224]{1,0:T(8,128)(2,1)S(1)} %collective-permute-done.1), channel_id=1, source_target_pairs={{0,2},{1,5},{2,0},{3,7},{4,6},{5,1},{6,4},{7,3},{8,10},{9,13},{10,... | collective-permute-start | bytes 304136 | tf_op jit(solution)/shard_map/ppermute | solution.py:74
  17.5 2.6 %collective-permute-start.8 = (bf16[34,4096]{1,0:T(8,128)(2,1)S(1)}, bf16[34,4096]{1,0:T(8,128)(2,1)S(1)}, u32[]{:S(2)}, u32[]{:S(2)}) collective-permute-start(bf16[34,4096]{1,0:T(8,128)(2,1)S(1)} %get-tuple-element.36), channel_id=1, source_target_pairs={{0,8},{1,9},{2,10},{3,11},{4,12},{5,13},{6,14},{7,15},{8,0},{9,1},... | collective-permute-start | bytes 835592 | tf_op jit(solution)/shard_map/ppermute | solution.py:74
  20.1 0.9 %collective-permute-done.4 = bf16[12,4224]{1,0:T(8,128)(2,1)S(1)} collective-permute-done((bf16[12,4224]{1,0:T(8,128)(2,1)S(1)}, bf16[12,4224]{1,0:T(8,128)(2,1)S(1)}, u32[]{:S(2)}, u32[]{:S(2)}) %collective-permute-start.4) | collective-permute-done | bytes 101408 | tf_op jit(solution)/shard_map/ppermute | solution.py:74
  21.1 1.9 %collective-permute-start.7 = (bf16[24,4224]{1,0:T(8,128)(2,1)S(1)}, bf16[24,4224]{1,0:T(8,128)(2,1)S(1)}, u32[]{:S(2)}, u32[]{:S(2)}) collective-permute-start(bf16[24,4224]{1,0:T(8,128)(2,1)S(1)} %pad_maximum_fusion.1.refs_1_), channel_id=1, source_target_pairs={{0,4},{1,3},{2,6},{3,1},{4,0},{5,7},{6,2},{7,5},{8,12},{9,11},{10,... | collective-permute-start | bytes 608264 | tf_op jit(solution)/shard_map/ppermute | solution.py:74
  23.1 1.3 %collective-permute-done.10.refs_7_ = bf16[24,4096]{1,0:T(8,128)(2,1)S(1)} collective-permute-done((bf16[24,4096]{1,0:T(8,128)(2,1)S(1)}, bf16[24,4096]{1,0:T(8,128)(2,1)S(1)}, u32[]{:S(2)}, u32[]{:S(2)}) %collective-permute-start.10) | collective-permute-done | bytes 196640 | tf_op jit(solution)/shard_map/ppermute | solution.py:78
  24.4 2.5 %collective-permute-done.7.refs_3_ = bf16[24,4224]{1,0:T(8,128)(2,1)S(1)} collective-permute-done((bf16[24,4224]{1,0:T(8,128)(2,1)S(1)}, bf16[24,4224]{1,0:T(8,128)(2,1)S(1)}, u32[]{:S(2)}, u32[]{:S(2)}) %collective-permute-start.7) | collective-permute-done | bytes 202784 | tf_op jit(solution)/shard_map/ppermute | solution.py:74
  26.9 1.8 %partials.2 = (f32[4,48]{1,0:T(4,128)S(1)}, f32[4,48]{1,0:T(4,128)S(1)}) custom-call(bf16[24,4224]{1,0:T(8,128)(2,1)S(1)} %pad_maximum_fusion.refs_0_, bf16[24,4224]{1,0:T(8,128)(2,1)S(1)} %pad_maximum_fusion.1.refs_1_, bf16[24,4224]{1,0:T(8,128)(2,1)S(1)} %collective-permute-done.5.refs_2_, bf16[24,4224]{1,0:T(8,128)(2,1)S(1)} %collective-permute-done.7.refs_3_, ...), custom_call_target="tpu_custom_call" | custom-call | tf_op jit(solution)/shard_map/partials/pallas_call | solution.py:241
  28.8 1.6 %collective-permute-done.12.refs_5_ = bf16[34,4096]{1,0:T(8,128)(2,1)S(1)} collective-permute-done((bf16[34,4096]{1,0:T(8,128)(2,1)S(1)}, bf16[34,4096]{1,0:T(8,128)(2,1)S(1)}, u32[]{:S(2)}, u32[]{:S(2)}) %collective-permute-start.12) | collective-permute-done | bytes 278560 | tf_op jit(solution)/shard_map/ppermute | solution.py:78
  30.4 0.8 %partials.3 = (f32[4,48]{1,0:T(4,128)S(1)}, f32[4,48]{1,0:T(4,128)S(1)}) custom-call(bf16[24,4224]{1,0:T(8,128)(2,1)S(1)} %pad_maximum_fusion.refs_0_, bf16[24,4224]{1,0:T(8,128)(2,1)S(1)} %pad_maximum_fusion.1.refs_1_, bf16[24,4224]{1,0:T(8,128)(2,1)S(1)} %collective-permute-done.5.refs_2_, bf16[24,4224]{1,0:T(8,128)(2,1)S(1)} %collective-permute-done.7.refs_3_, ...), custom_call_target="tpu_custom_call" | custom-call | tf_op jit(solution)/shard_map/partials/pallas_call | solution.py:241
  31.1 1.8 %collective-permute-start.13 = (f32[4,48]{1,0:T(4,128)S(1)}, f32[4,48]{1,0:T(4,128)S(1)}, u32[]{:S(2)}, u32[]{:S(2)}) collective-permute-start(f32[4,48]{1,0:T(4,128)S(1)} %get-tuple-element.45), channel_id=1, source_target_pairs={{0,4},{1,3},{2,6},{3,1},{4,0},{5,7},{6,2},{7,5},{8,12},{9,11},{10,... | collective-permute-start | bytes 2312 | tf_op jit(solution)/shard_map/ppermute | solution.py:74
  33.0 1.8 %collective-permute-done.13.theirs_ref = f32[4,48]{1,0:T(4,128)S(1)} collective-permute-done((f32[4,48]{1,0:T(4,128)S(1)}, f32[4,48]{1,0:T(4,128)S(1)}, u32[]{:S(2)}, u32[]{:S(2)}) %collective-permute-start.13) | collective-permute-done | bytes 800 | tf_op jit(solution)/shard_map/ppermute | solution.py:74
  34.8 1.8 %collective-permute-start.14 = (f32[4,24]{1,0:T(4,128)S(1)}, f32[4,24]{1,0:T(4,128)S(1)}, u32[]{:S(2)}, u32[]{:S(2)}) collective-permute-start(f32[4,24]{1,0:T(4,128)S(1)} %get-tuple-element.47), channel_id=1, source_target_pairs={{0,2},{1,5},{2,0},{3,7},{4,6},{5,1},{6,4},{7,3},{8,10},{9,13},{10,... | collective-permute-start | bytes 1160 | tf_op jit(solution)/shard_map/ppermute | solution.py:74
  36.7 1.8 %collective-permute-done.14.theirs_ref = f32[4,24]{1,0:T(4,128)S(1)} collective-permute-done((f32[4,24]{1,0:T(4,128)S(1)}, f32[4,24]{1,0:T(4,128)S(1)}, u32[]{:S(2)}, u32[]{:S(2)}) %collective-permute-start.14) | collective-permute-done | bytes 416 | tf_op jit(solution)/shard_map/ppermute | solution.py:74
  38.6 2.8 %collective-permute-start.15 = (f32[4,12]{1,0:T(4,128)S(1)}, f32[4,12]{1,0:T(4,128)S(1)}, u32[]{:S(2)}, u32[]{:S(2)}) collective-permute-start(f32[4,12]{1,0:T(4,128)S(1)} %get-tuple-element.49), channel_id=1, source_target_pairs={{0,16},{1,17},{2,18},{3,19},{4,20},{5,21},{6,22},{7,23},{8,24},{9,... | collective-permute-start | bytes 584 | tf_op jit(solution)/shard_map/ppermute | solution.py:74
  41.4 1.7 %collective-permute-done.15.theirs_ref = f32[4,12]{1,0:T(4,128)S(1)} collective-permute-done((f32[4,12]{1,0:T(4,128)S(1)}, f32[4,12]{1,0:T(4,128)S(1)}, u32[]{:S(2)}, u32[]{:S(2)}) %collective-permute-start.15) | collective-permute-done | bytes 224 | tf_op jit(solution)/shard_map/ppermute | solution.py:74
  43.2 1.1 %collective-permute-done.16 = f32[2,12]{1,0:T(2,128)S(1)} collective-permute-done((f32[2,12]{1,0:T(2,128)S(1)}, f32[2,12]{1,0:T(2,128)S(1)}, u32[]{:S(2)}, u32[]{:S(2)}) %collective-permute-start.16) | collective-permute-done | bytes 128 | tf_op jit(solution)/shard_map/ppermute | solution.py:78
  44.4 0.5 %slice_bitcast_fusion = (f32[24]{0:T(128)}, f32[24]{0:T(128)}) fusion(f32[2,24]{1,0:T(2,128)S(1)} %fusion.2), kind=kLoop, calls=%fused_computation.8 | loop fusion | bytes 384 | tf_op jit(solution)/shard_map/squeeze | solution.py:337
  (28 shorter events, 1.4 us)
Async XLA Ops:
  0.6 4.6 %collective-permute-start = (bf16[24,2048]{1,0:T(8,128)(2,1)}, bf16[24,2048]{1,0:T(8,128)(2,1)S(1)}, u32[]{:S(2)}, u32[]{:S(2)}) collective-permute-start(bf16[24,2048]{1,0:T(8,128)(2,1)} %hidden_in.1), channel_id=1, source_target_pairs={{0,1},{1,0},{2,3},{3,2},{4,5},{5,4},{6,7},{7,6},{8,9},{9,8},{10,11... | collective-permute-start | bytes 294920 | tf_op jit(solution)/shard_map/ppermute | solution.py:78
  1.2 16.3 %copy-start = (bf16[98,4096]{1,0:T(8,128)(2,1)S(1)}, bf16[98,4096]{1,0:T(8,128)(2,1)}, u32[]{:S(2)}) copy-start(bf16[98,4096]{1,0:T(8,128)(2,1)} %refs_4_.1) | copy-start | bytes 2408452
  2.6 11.3 %collective-permute-start.3 = (bf16[24,4096]{1,0:T(8,128)(2,1)S(1)}, bf16[24,4096]{1,0:T(8,128)(2,1)S(1)}, u32[]{:S(2)}, u32[]{:S(2)}) collective-permute-start(bf16[24,4096]{1,0:T(8,128)(2,1)S(1)} %get-tuple-element.30), channel_id=1, source_target_pairs={{0,8},{1,9},{2,10},{3,11},{4,12},{5,13},{6,14},{7,15},{8,0},{9,1},... | collective-permute-start | bytes 589832 | tf_op jit(solution)/shard_map/ppermute | solution.py:74
  5.4 8.4 %collective-permute-start.1 = (bf16[12,4224]{1,0:T(8,128)(2,1)S(1)}, bf16[12,4224]{1,0:T(8,128)(2,1)S(1)}, u32[]{:S(2)}, u32[]{:S(2)}) collective-permute-start(bf16[12,4224]{1,0:T(8,128)(2,1)S(1)} %normalize_rows.1), channel_id=1, source_target_pairs={{0,16},{1,17},{2,18},{3,19},{4,20},{5,21},{6,22},{7,23},{8,24},{9,... | collective-permute-start | bytes 304136 | tf_op jit(solution)/shard_map/ppermute | solution.py:74
  8.1 5.8 %collective-permute-start.2 = (bf16[12,4224]{1,0:T(8,128)(2,1)S(1)}, bf16[12,4224]{1,0:T(8,128)(2,1)S(1)}, u32[]{:S(2)}, u32[]{:S(2)}) collective-permute-start(bf16[12,4224]{1,0:T(8,128)(2,1)S(1)} %normalize_rows.1), channel_id=1, source_target_pairs={{0,2},{1,5},{2,0},{3,7},{4,6},{5,1},{6,4},{7,3},{8,10},{9,13},{10,... | collective-permute-start | bytes 304136 | tf_op jit(solution)/shard_map/ppermute | solution.py:74
  9.6 11.4 %collective-permute-start.6 = (bf16[40,4096]{1,0:T(8,128)(2,1)S(1)}, bf16[40,4096]{1,0:T(8,128)(2,1)S(1)}, u32[]{:S(2)}, u32[]{:S(2)}) collective-permute-start(bf16[40,4096]{1,0:T(8,128)(2,1)S(1)} %get-tuple-element.33), channel_id=1, source_target_pairs={{0,8},{1,9},{2,10},{3,11},{4,12},{5,13},{6,14},{7,15},{8,0},{9,1},... | collective-permute-start | bytes 983048 | tf_op jit(solution)/shard_map/ppermute | solution.py:74
  13.9 7.1 %collective-permute-start.5 = (bf16[24,4224]{1,0:T(8,128)(2,1)S(1)}, bf16[24,4224]{1,0:T(8,128)(2,1)S(1)}, u32[]{:S(2)}, u32[]{:S(2)}) collective-permute-start(bf16[24,4224]{1,0:T(8,128)(2,1)S(1)} %pad_maximum_fusion.refs_0_), channel_id=1, source_target_pairs={{0,4},{1,3},{2,6},{3,1},{4,0},{5,7},{6,2},{7,5},{8,12},{9,11},{10,... | collective-permute-start | bytes 608264 | tf_op jit(solution)/shard_map/ppermute | solution.py:74
  16.0 5.0 %collective-permute-start.4 = (bf16[12,4224]{1,0:T(8,128)(2,1)S(1)}, bf16[12,4224]{1,0:T(8,128)(2,1)S(1)}, u32[]{:S(2)}, u32[]{:S(2)}) collective-permute-start(bf16[12,4224]{1,0:T(8,128)(2,1)S(1)} %collective-permute-done.1), channel_id=1, source_target_pairs={{0,2},{1,5},{2,0},{3,7},{4,6},{5,1},{6,4},{7,3},{8,10},{9,13},{10,... | collective-permute-start | bytes 304136 | tf_op jit(solution)/shard_map/ppermute | solution.py:74
  17.5 9.4 %collective-permute-start.9 = (bf16[98,4096]{1,0:T(8,128)(2,1)S(1)}, bf16[98,4096]{1,0:T(8,128)(2,1)S(1)}, u32[]{:S(2)}, u32[]{:S(2)}) collective-permute-start(bf16[98,4096]{1,0:T(8,128)(2,1)S(1)} %copy-done), channel_id=1, source_target_pairs={{0,1},{1,0},{2,3},{3,2},{4,5},{5,4},{6,7},{7,6},{8,9},{9,8},{10,11... | collective-permute-start | bytes 2408456 | tf_op jit(solution)/shard_map/ppermute | solution.py:78
  17.5 11.3 %collective-permute-start.8 = (bf16[34,4096]{1,0:T(8,128)(2,1)S(1)}, bf16[34,4096]{1,0:T(8,128)(2,1)S(1)}, u32[]{:S(2)}, u32[]{:S(2)}) collective-permute-start(bf16[34,4096]{1,0:T(8,128)(2,1)S(1)} %get-tuple-element.36), channel_id=1, source_target_pairs={{0,8},{1,9},{2,10},{3,11},{4,12},{5,13},{6,14},{7,15},{8,0},{9,1},... | collective-permute-start | bytes 835592 | tf_op jit(solution)/shard_map/ppermute | solution.py:74
  21.0 5.9 %collective-permute-start.11 = (bf16[40,4096]{1,0:T(8,128)(2,1)S(1)}, bf16[40,4096]{1,0:T(8,128)(2,1)S(1)}, u32[]{:S(2)}, u32[]{:S(2)}) collective-permute-start(bf16[40,4096]{1,0:T(8,128)(2,1)S(1)} %collective-permute-done.6.refs_8_), channel_id=1, source_target_pairs={{0,1},{1,0},{2,3},{3,2},{4,5},{5,4},{6,7},{7,6},{8,9},{9,8},{10,11... | collective-permute-start | bytes 983048 | tf_op jit(solution)/shard_map/ppermute | solution.py:78
  21.1 5.8 %collective-permute-start.7 = (bf16[24,4224]{1,0:T(8,128)(2,1)S(1)}, bf16[24,4224]{1,0:T(8,128)(2,1)S(1)}, u32[]{:S(2)}, u32[]{:S(2)}) collective-permute-start(bf16[24,4224]{1,0:T(8,128)(2,1)S(1)} %pad_maximum_fusion.1.refs_1_), channel_id=1, source_target_pairs={{0,4},{1,3},{2,6},{3,1},{4,0},{5,7},{6,2},{7,5},{8,12},{9,11},{10,... | collective-permute-start | bytes 608264 | tf_op jit(solution)/shard_map/ppermute | solution.py:74
  23.0 1.4 %collective-permute-start.10 = (bf16[24,4096]{1,0:T(8,128)(2,1)S(1)}, bf16[24,4096]{1,0:T(8,128)(2,1)S(1)}, u32[]{:S(2)}, u32[]{:S(2)}) collective-permute-start(bf16[24,4096]{1,0:T(8,128)(2,1)S(1)} %collective-permute-done.3.refs_6_), channel_id=1, source_target_pairs={{0,1},{1,0},{2,3},{3,2},{4,5},{5,4},{6,7},{7,6},{8,9},{9,8},{10,11... | collective-permute-start | bytes 589832 | tf_op jit(solution)/shard_map/ppermute | solution.py:78
  28.7 1.6 %collective-permute-start.12 = (bf16[34,4096]{1,0:T(8,128)(2,1)S(1)}, bf16[34,4096]{1,0:T(8,128)(2,1)S(1)}, u32[]{:S(2)}, u32[]{:S(2)}) collective-permute-start(bf16[34,4096]{1,0:T(8,128)(2,1)S(1)} %collective-permute-done.8.refs_4_), channel_id=1, source_target_pairs={{0,1},{1,0},{2,3},{3,2},{4,5},{5,4},{6,7},{7,6},{8,9},{9,8},{10,11... | collective-permute-start | bytes 835592 | tf_op jit(solution)/shard_map/ppermute | solution.py:78
  31.1 3.6 %collective-permute-start.13 = (f32[4,48]{1,0:T(4,128)S(1)}, f32[4,48]{1,0:T(4,128)S(1)}, u32[]{:S(2)}, u32[]{:S(2)}) collective-permute-start(f32[4,48]{1,0:T(4,128)S(1)} %get-tuple-element.45), channel_id=1, source_target_pairs={{0,4},{1,3},{2,6},{3,1},{4,0},{5,7},{6,2},{7,5},{8,12},{9,11},{10,... | collective-permute-start | bytes 2312 | tf_op jit(solution)/shard_map/ppermute | solution.py:74
  34.8 1.8 %copy-start.1 = (s32[3]{0:T(128)S(1)}, s32[3]{0:T(128)}, u32[]{:S(2)}) copy-start(s32[3]{0:T(128)} %param.13) | copy-start | bytes 40
  34.8 1.8 %copy-start.2 = (s32[3]{0:T(128)S(1)}, s32[3]{0:T(128)}, u32[]{:S(2)}) copy-start(s32[3]{0:T(128)} %param.12) | copy-start | bytes 40
  34.8 3.7 %collective-permute-start.14 = (f32[4,24]{1,0:T(4,128)S(1)}, f32[4,24]{1,0:T(4,128)S(1)}, u32[]{:S(2)}, u32[]{:S(2)}) collective-permute-start(f32[4,24]{1,0:T(4,128)S(1)} %get-tuple-element.47), channel_id=1, source_target_pairs={{0,2},{1,5},{2,0},{3,7},{4,6},{5,1},{6,4},{7,3},{8,10},{9,13},{10,... | collective-permute-start | bytes 1160 | tf_op jit(solution)/shard_map/ppermute | solution.py:74
  38.6 4.5 %collective-permute-start.15 = (f32[4,12]{1,0:T(4,128)S(1)}, f32[4,12]{1,0:T(4,128)S(1)}, u32[]{:S(2)}, u32[]{:S(2)}) collective-permute-start(f32[4,12]{1,0:T(4,128)S(1)} %get-tuple-element.49), channel_id=1, source_target_pairs={{0,16},{1,17},{2,18},{3,19},{4,20},{5,21},{6,22},{7,23},{8,24},{9,... | collective-permute-start | bytes 584 | tf_op jit(solution)/shard_map/ppermute | solution.py:74
  43.1 1.2 %collective-permute-start.16 = (f32[2,12]{1,0:T(2,128)S(1)}, f32[2,12]{1,0:T(2,128)S(1)}, u32[]{:S(2)}, u32[]{:S(2)}) collective-permute-start(f32[2,12]{1,0:T(2,128)S(1)} %finish.1), channel_id=1, source_target_pairs={{0,1},{1,0},{2,3},{3,2},{4,5},{5,4},{6,7},{7,6},{8,9},{9,8},{10,11... | collective-permute-start | bytes 296 | tf_op jit(solution)/shard_map/ppermute | solution.py:78

commit v3 on v2

--- a/solution.py
+++ b/solution.py
@@ -99,14 +99,12 @@
     for copy in copies:
         copy.start()
     copies[0].wait()
-    core = lax.axis_index("tp")
-    row = lax.broadcasted_iota(jnp.int32, (half, LANES), 0)
+    slots = ids_ref.shape[1]
+    slot = lax.axis_index("tp") * half + lax.broadcasted_iota(jnp.int32, (half, slots), 0)
+    column = lax.broadcasted_iota(jnp.int32, (half, slots), 1)
+    row_ids = jnp.where(slot == column, ids_ref[...], 0).sum(axis=1, keepdims=True)
     lane = lax.broadcasted_iota(jnp.int32, (half, LANES), 1)
-    digits = jnp.zeros((half, LANES), jnp.int32)
-    for index in range(half):
-        row_id = ids_ref[core * half + index]
-        digit = jnp.where(lane == 0, row_id >> 8, jnp.where(lane == 1, row_id & 255, 0))
-        digits = jnp.where(row == index, digit, digits)
+    digits = jnp.where(lane == 0, row_ids >> 8, jnp.where(lane == 1, row_ids & 255, 0))
     digit_ref[...] = digits.astype(jnp.float32).astype(jnp.bfloat16)
     for copy in copies[1:]:
         copy.wait()
@@ -135,14 +133,21 @@
         in_specs=[pl.BlockSpec(memory_space=pltpu.HBM)] * 5,
         out_specs=[vmem] * (4 + len(chunks)),
         scratch_shapes=[
-            pltpu.SMEM(targets.shape, jnp.int32),
+            pltpu.VMEM((1, targets.shape[0]), jnp.int32),
             pltpu.SemaphoreType.DMA((4 + len(chunks),)),
         ],
         compiler_params=pltpu.CompilerParams(vmem_limit_bytes=KERNEL_VMEM),
         name="stage",
     )(
         *map(
-            in_hbm, (hidden, norm_gain.reshape(1, -1), norm_bias.reshape(1, -1), unembed, targets)
+            in_hbm,
+            (
+                hidden,
+                norm_gain.reshape(1, -1),
+                norm_bias.reshape(1, -1),
+                unembed,
+                targets.reshape(1, -1),
+            ),
         )
     )
 
@@ -187,26 +192,21 @@
     return top, total, spread, one[3] + two[3]
 
 
-def partials_kernel(places, vocab_part, pieces, *refs):
-    count = len(places)
-    piece_refs, blocks = refs[:pieces], refs[pieces : pieces + count]
-    earlier, outs, rows_ref = refs[pieces + count : -3], refs[-3:-1], refs[-1]
+CONTRACT = (((1,), (1,)), ((), ()))
+
+
+def block_stats(rows_ref, blocks, places, vocab_part):
     width = blocks[0].shape[1]
     row_count = rows_ref.shape[0]
-    piece_rows = row_count // pieces
-    for index, piece in enumerate(piece_refs):
-        rows_ref[pl.ds(index * piece_rows, piece_rows), :] = piece[...]
     chip, core = lax.axis_index("req"), lax.axis_index("tp")
-
     lane = lax.broadcasted_iota(jnp.int32, (16, LANES), 1)
     pick = jnp.where(lane == 0, 256.0, jnp.where(lane == 1, 1.0, 0.0)).astype(jnp.bfloat16)
-    contract = (((1,), (1,)), ((), ()))
     row_ids = lax.dot_general(
-        pick, rows_ref[:, pl.ds(width, LANES)], contract, preferred_element_type=jnp.float32
+        pick, rows_ref[:, pl.ds(width, LANES)], CONTRACT, preferred_element_type=jnp.float32
     )[:1].astype(jnp.int32)
     rows = rows_ref[:, pl.ds(0, width)]
     scores = [
-        lax.dot_general(block[...], rows, contract, preferred_element_type=jnp.float32)
+        lax.dot_general(block[...], rows, CONTRACT, preferred_element_type=jnp.float32)
         for block in blocks
     ]
     top = scores[0].max(axis=0, keepdims=True)
@@ -214,47 +214,93 @@
         top = jnp.maximum(top, part.max(axis=0, keepdims=True))
     total = jnp.zeros((1, row_count), jnp.float32)
     spread, hit = total, total
-    for part, (chip_bit, core_bit, start) in zip(scores, places):
+    for part, (chip_bit, start) in zip(scores, places):
         shifted = part - top
         weights = jnp.exp(shifted)
         total += weights.sum(axis=0, keepdims=True)
         spread += (weights * shifted).sum(axis=0, keepdims=True)
-        first = ((chip ^ chip_bit) * 2 + (core ^ core_bit)) * vocab_part + start
+        first = ((chip ^ chip_bit) * 2 + core) * vocab_part + start
         ids = first + lax.broadcasted_iota(jnp.int32, (part.shape[0], 1), 0)
         hit += jnp.where(ids == row_ids, part, 0.0).sum(axis=0, keepdims=True)
-    stats = (top, total, spread, hit)
-    half = row_count // 2
-    if earlier:
-        before = [
-            jnp.concatenate([ref[pl.ds(k, 1), :] for ref in earlier], axis=1) for k in range(4)
-        ]
-        stats = merge(before, stats)
+    return top, total, spread, hit
+
+
+def lay(pieces, rows_ref):
+    at = 0
+    for piece in pieces:
+        rows_ref[pl.ds(at, piece.shape[0]), :] = piece[...]
+        at += piece.shape[0]
+
+
+def early_kernel(places, vocab_part, pieces, *refs):
+    stats_ref, rows_ref = refs[-2:]
+    lay(refs[:pieces], rows_ref)
+    stats = block_stats(rows_ref, refs[pieces:-2], places, vocab_part)
     for k in range(4):
-        outs[0][pl.ds(k, 1), :] = stats[k][:, :half]
-        outs[1][pl.ds(k, 1), :] = stats[k][:, half:]
-
-
-def partials(rows, blocks, places, vocab_part, earlier=()):
-    row_count = len(rows) * rows[0].shape[0]
-    half = row_count // 2
-    vmem = pl.BlockSpec(memory_space=pltpu.VMEM)
-    return pl.pallas_call(
-        functools.partial(partials_kernel, places, vocab_part, len(rows)),
-        out_shape=[pltpu.VMEM((4, half), jnp.float32)] * 2,
-        in_specs=[vmem] * (len(rows) + len(blocks) + len(earlier)),
+        stats_ref[pl.ds(k, 1), :] = stats[k]
+
+
+def late_kernel(places, vocab_part, early_ref, rows_ref, mine_ref, other_ref, *refs):
+    blocks, stats_ref, last_rows_ref = refs[:-2], refs[-2], refs[-1]
+    lay((mine_ref, other_ref), last_rows_ref)
+    new = block_stats(last_rows_ref, blocks, places, vocab_part)
+    rest = block_stats(rows_ref, blocks[-1:], places[-1:], vocab_part)
+    old = merge([early_ref[pl.ds(k, 1), :] for k in range(4)], rest)
+    old_half, new_half = old[0].shape[1] // 2, new[0].shape[1] // 2
+    for k in range(4):
+        stats_ref[pl.ds(k, 1), :] = jnp.concatenate(
+            [
+                old[k][:, :old_half],
+                new[k][:, :new_half],
+                old[k][:, old_half:],
+                new[k][:, new_half:],
+            ],
+            axis=1,
+        )
+
+
+def early_partials(pieces, blocks, places, vocab_part):
+    row_count = len(pieces) * pieces[0].shape[0]
+    vmem = pl.BlockSpec(memory_space=pltpu.VMEM)
+    return pl.pallas_call(
+        functools.partial(early_kernel, places, vocab_part, len(pieces)),
+        out_shape=[
+            pltpu.VMEM((4, row_count), jnp.float32),
+            pltpu.VMEM((row_count, pieces[0].shape[1]), jnp.bfloat16),
+        ],
+        in_specs=[vmem] * (len(pieces) + len(blocks)),
         out_specs=[vmem] * 2,
-        scratch_shapes=[pltpu.VMEM((row_count, rows[0].shape[1]), jnp.bfloat16)],
-        compiler_params=pltpu.CompilerParams(vmem_limit_bytes=KERNEL_VMEM),
-        name="partials",
-    )(*map(in_vmem, (*rows, *blocks, *earlier)))
-
-
-def merge_kernel(group, mine_ref, theirs_ref, keep_ref, give_ref):
-    mine, theirs = ([ref[pl.ds(k, 1), :] for k in range(4)] for ref in (mine_ref, theirs_ref))
+        compiler_params=pltpu.CompilerParams(vmem_limit_bytes=KERNEL_VMEM),
+        name="early_partials",
+    )(*map(in_vmem, (*pieces, *blocks)))
+
+
+def late_partials(early, rows, mine, other, blocks, places, vocab_part):
+    last_count = 2 * mine.shape[0]
+    vmem = pl.BlockSpec(memory_space=pltpu.VMEM)
+    return pl.pallas_call(
+        functools.partial(late_kernel, places, vocab_part),
+        out_shape=pltpu.VMEM((4, rows.shape[0] + last_count), jnp.float32),
+        in_specs=[vmem] * (4 + len(blocks)),
+        out_specs=vmem,
+        scratch_shapes=[pltpu.VMEM((last_count, rows.shape[1]), jnp.bfloat16)],
+        compiler_params=pltpu.CompilerParams(vmem_limit_bytes=KERNEL_VMEM),
+        name="late_partials",
+    )(*map(in_vmem, (early, rows, mine, other, *blocks)))
+
+
+def blocks_of(value, group, order):
+    return jnp.concatenate([value[:, at * group : (at + 1) * group] for at in order], axis=1)
+
+
+def merge_kernel(group, theirs_order, orders, mine_ref, theirs_ref, *outs):
+    mine = [mine_ref[pl.ds(k, 1), :] for k in range(4)]
+    theirs = [theirs_ref[pl.ds(k, 1), :] for k in range(4)]
+    if theirs_order:
+        theirs = [blocks_of(value, group, theirs_order) for value in theirs]
     for k, value in enumerate(merge(mine, theirs)):
-        pieces = [value[:, at : at + group] for at in range(0, value.shape[1], group)]
-        keep_ref[pl.ds(k, 1), :] = jnp.concatenate(pieces[0::2], axis=1)
-        give_ref[pl.ds(k, 1), :] = jnp.concatenate(pieces[1::2], axis=1)
+        for out, order in zip(outs, orders):
+            out[pl.ds(k, 1), :] = blocks_of(value, group, order)
 
 
 def finish_kernel(mine_ref, theirs_ref, out_ref):
@@ -265,13 +311,13 @@
     out_ref[pl.ds(1, 1), :] = log_total - row_spread / row_total
 
 
-def merge_and_split(mine, theirs, group):
-    vmem = pl.BlockSpec(memory_space=pltpu.VMEM)
-    return pl.pallas_call(
-        functools.partial(merge_kernel, group),
-        out_shape=[pltpu.VMEM((4, mine.shape[1] // 2), jnp.float32)] * 2,
+def merge_and_split(mine, theirs, group, orders, theirs_order=()):
+    vmem = pl.BlockSpec(memory_space=pltpu.VMEM)
+    return pl.pallas_call(
+        functools.partial(merge_kernel, group, theirs_order, orders),
+        out_shape=[pltpu.VMEM((4, group * len(order)), jnp.float32) for order in orders],
         in_specs=[vmem] * 2,
-        out_specs=[vmem] * 2,
+        out_specs=[vmem] * len(orders),
         compiler_params=pltpu.CompilerParams(vmem_limit_bytes=KERNEL_VMEM),
         name="merge_and_split",
     )(in_vmem(mine), in_vmem(theirs))
@@ -311,26 +357,28 @@
     far_side, near_across, near[1] = lax.optimization_barrier((far_side, near_across, near[1]))
     far_rows = jnp.concatenate([far, far_side], axis=0)
     far_across = exchange(far_rows, SECOND)
-
-    blocks, places = [unembed, core_swap(unembed)], [(0, 0, 0), (0, 1, 0)]
-    for block, start in zip(near, cuts):
-        if start != cuts[-2]:
-            blocks += [block, core_swap(block)]
-            places += [(Z_NEAR, 0, start), (Z_NEAR, 1, start)]
-    rows = [near_rows, far_rows, near_across, far_across]
-    early = partials(rows, blocks, places, vocab_part)
-    last, early = lax.optimization_barrier((near[-1], early))
-    blocks = [last, core_swap(last)]
-    places = [(Z_NEAR, core_bit, cuts[-2]) for core_bit in (0, 1)]
-    keep, give = partials(rows, blocks, places, vocab_part, early)
-    keep, give = merge_and_split(keep, exchange(give, SECOND), half)
-    keep, give = merge_and_split(keep, exchange(give, FIRST), half)
+    far_across, near[2] = lax.optimization_barrier((far_across, near[2]))
+    blocks, places = [unembed, *near], [(0, 0)] + [(Z_NEAR, start) for start in cuts[:-1]]
+    pieces = [near_rows, far_rows, near_across]
+    pieces += [core_swap(piece) for piece in pieces]
+    early, rows = early_partials(pieces, blocks[:-1], places[:-1], vocab_part)
+    other_across = core_swap(far_across)
+    stats = late_partials(early, rows, far_across, other_across, blocks, places, vocab_part)
+    swapped = (*range(8, 16), *range(8))
+    keep, give = merge_and_split(
+        stats,
+        core_swap(stats),
+        half,
+        ((0, 1, 2, 3, 8, 10, 12, 14), (4, 5, 6, 7, 9, 11, 13, 15)),
+        swapped,
+    )
+    keep, give = merge_and_split(
+        keep, exchange(give, SECOND), half, ((0, 2, 4, 5), (1, 3, 6, 7))
+    )
+    keep, give = merge_and_split(keep, exchange(give, FIRST), half, ((0, 2), (1, 3)))
     result = finish(keep, exchange(give, FAR))
-    partner = core_swap(result)
     both = jnp.where(
-        first_core,
-        jnp.concatenate([result, partner], axis=1),
-        jnp.concatenate([partner, result], axis=1),
+        first_core, result, jnp.concatenate([result[:, half:], result[:, :half]], axis=1)
     )
     live = live_mask(span_start, span_end, slot_count)
     both = jnp.where(live, both, 0.0)

time: 45 us -> 44.7 us (level)
  waiting for transfers between devices: 16.6 us -> 15.3 us
  starting transfers between devices: 22.4 us -> 23.2 us
    ppermute x6, waiting for transfers between devices: 4.07 us -> 0.9 us  [core_swap(): return lax.ppermute(value, 'tp', [(0, 1), (1, 0)])]
    ppermute x11, waiting for transfers between devices: 12.5 us -> 14.4 us  [exchange(): return lax.ppermute(value, ('req', 'tp'), pairs)]
    ppermute x6, starting transfers between devices: 0.8 us -> 1.59 us  [core_swap(): return lax.ppermute(value, 'tp', [(0, 1), (1, 0)])]
    pallas_call x4 -> x5, Pallas kernels: 2.74 us -> 2.86 us  [the longest x1 1.34 us: early_partials(): pl.pallas_call(functools.partial(early_kernel, places, vocab_part, len(pi...]
  transfers between devices with their start and end apart: 17 -> 17, of which waited for: 9 -> 8; matrix products, arithmetic and copies ran while one was open for 0% -> 0% of each run, Pallas kernels for 8% -> 6%
where the time goes in v3:
time: 44.7 us; the launch traced here: 44.6 us
  starting transfers between devices  23.2 us (52%)
  waiting for transfers between devices  15.3 us (34%)
  Pallas kernels  4.4 us (10%)
  between operations  0.74 us (2%)
  local copies, waits for them, and re-layouts  0.61 us (1%)
    ppermute x11, starting transfers between devices, exchange(): return lax.ppermute(value, ('req', 'tp'), pairs)  21.6 us
    ppermute x11, waiting for transfers between devices, exchange(): return lax.ppermute(value, ('req', 'tp'), pairs)  14.4 us
    ppermute x6, starting transfers between devices, core_swap(): return lax.ppermute(value, 'tp', [(0, 1), (1, 0)])  1.59 us
    pallas_call x1, Pallas kernels, early_partials(): pl.pallas_call(functools.partial(early_kernel, places, vocab_part, len(pi...  1.34 us
    pallas_call x1, Pallas kernels, stage(): pl.pallas_call(functools.partial(stage_kernel, cuts, half), out_shape=[pl...  1.33 us
    pallas_call x1, Pallas kernels, late_partials(): pl.pallas_call(functools.partial(late_kernel, places, vocab_part), out_sh...  1.19 us
    ppermute x6, waiting for transfers between devices, core_swap(): return lax.ppermute(value, 'tp', [(0, 1), (1, 0)])  0.9 us
  transfers between devices with their start and end apart: 17, of which 8 were waited for; matrix products, arithmetic and copies ran while one was open for 0% of the time, Pallas kernels for 6%

profile of v3, /device:TPU:0, one launch (start us, length us, event | category | flops | bytes accessed | tf_op | source)
XLA Modules:
  0.0 44.6 jit_solution(17095418645894420481)
XLA Ops:
  0.6 0.6 %collective-permute-start = (bf16[24,2048]{1,0:T(8,128)(2,1)}, bf16[24,2048]{1,0:T(8,128)(2,1)S(1)}, u32[]{:S(2)}, u32[]{:S(2)}) collective-permute-start(bf16[24,2048]{1,0:T(8,128)(2,1)} %hidden_in.1), channel_id=1, source_target_pairs={{0,1},{1,0},{2,3},{3,2},{4,5},{5,4},{6,7},{7,6},{8,9},{9,8},{10,11... | collective-permute-start | bytes 294920 | tf_op jit(solution)/shard_map/ppermute | solution.py:78
  1.2 1.3 %stage.1 = (bf16[24,2048]{1,0:T(8,128)(2,1)S(1)}, f32[1,4096]{1,0:T(1,128)S(1)}, f32[1,4096]{1,0:T(1,128)S(1)}, bf16[12,128]{1,0:T(8,128)(2,1)S(1)}, bf16[24,409...) custom-call(bf16[24,2048]{1,0:T(8,128)(2,1)} %hidden_in.1, f32[1,4096]{1,0:T(1,128)} %bitcast.7, ...), custom_call_target="tpu_custom_call" | custom-call | tf_op jit(solution)/shard_map/stage/pallas_call | solution.py:124
  2.5 2.7 %collective-permute-start.3 = (bf16[24,4096]{1,0:T(8,128)(2,1)S(1)}, bf16[24,4096]{1,0:T(8,128)(2,1)S(1)}, u32[]{:S(2)}, u32[]{:S(2)}) collective-permute-start(bf16[24,4096]{1,0:T(8,128)(2,1)S(1)} %get-tuple-element.29), channel_id=1, source_target_pairs={{0,8},{1,9},{2,10},{3,11},{4,12},{5,13},{6,14},{7,15},{8,0},{9,1},... | collective-permute-start | bytes 589832 | tf_op jit(solution)/shard_map/ppermute | solution.py:74
  5.4 2.7 %collective-permute-start.1 = (bf16[12,4224]{1,0:T(8,128)(2,1)S(1)}, bf16[12,4224]{1,0:T(8,128)(2,1)S(1)}, u32[]{:S(2)}, u32[]{:S(2)}) collective-permute-start(bf16[12,4224]{1,0:T(8,128)(2,1)S(1)} %normalize_rows.1), channel_id=1, source_target_pairs={{0,16},{1,17},{2,18},{3,19},{4,20},{5,21},{6,22},{7,23},{8,24},{9,... | collective-permute-start | bytes 304136 | tf_op jit(solution)/shard_map/ppermute | solution.py:74
  8.1 1.5 %collective-permute-start.2 = (bf16[12,4224]{1,0:T(8,128)(2,1)S(1)}, bf16[12,4224]{1,0:T(8,128)(2,1)S(1)}, u32[]{:S(2)}, u32[]{:S(2)}) collective-permute-start(bf16[12,4224]{1,0:T(8,128)(2,1)S(1)} %normalize_rows.1), channel_id=1, source_target_pairs={{0,2},{1,5},{2,0},{3,7},{4,6},{5,1},{6,4},{7,3},{8,10},{9,13},{10,... | collective-permute-start | bytes 304136 | tf_op jit(solution)/shard_map/ppermute | solution.py:74
  10.0 3.8 %collective-permute-done.3.refs_7_.refs_1_ = bf16[24,4096]{1,0:T(8,128)(2,1)S(1)} collective-permute-done((bf16[24,4096]{1,0:T(8,128)(2,1)S(1)}, bf16[24,4096]{1,0:T(8,128)(2,1)S(1)}, u32[]{:S(2)}, u32[]{:S(2)}) %collective-permute-start.3) | collective-permute-done | bytes 196640 | tf_op jit(solution)/shard_map/ppermute | solution.py:74
  13.9 2.0 %collective-permute-start.5 = (bf16[24,4224]{1,0:T(8,128)(2,1)S(1)}, bf16[24,4224]{1,0:T(8,128)(2,1)S(1)}, u32[]{:S(2)}, u32[]{:S(2)}) collective-permute-start(bf16[24,4224]{1,0:T(8,128)(2,1)S(1)} %pad_maximum_fusion.refs_0_), channel_id=1, source_target_pairs={{0,4},{1,3},{2,6},{3,1},{4,0},{5,7},{6,2},{7,5},{8,12},{9,11},{10,... | collective-permute-start | bytes 608264 | tf_op jit(solution)/shard_map/ppermute | solution.py:74
  16.0 1.5 %collective-permute-start.4 = (bf16[12,4224]{1,0:T(8,128)(2,1)S(1)}, bf16[12,4224]{1,0:T(8,128)(2,1)S(1)}, u32[]{:S(2)}, u32[]{:S(2)}) collective-permute-start(bf16[12,4224]{1,0:T(8,128)(2,1)S(1)} %collective-permute-done.1), channel_id=1, source_target_pairs={{0,2},{1,5},{2,0},{3,7},{4,6},{5,1},{6,4},{7,3},{8,10},{9,13},{10,... | collective-permute-start | bytes 304136 | tf_op jit(solution)/shard_map/ppermute | solution.py:74
  17.5 2.6 %collective-permute-start.11 = (bf16[34,4096]{1,0:T(8,128)(2,1)S(1)}, bf16[34,4096]{1,0:T(8,128)(2,1)S(1)}, u32[]{:S(2)}, u32[]{:S(2)}) collective-permute-start(bf16[34,4096]{1,0:T(8,128)(2,1)S(1)} %get-tuple-element.39), channel_id=1, source_target_pairs={{0,8},{1,9},{2,10},{3,11},{4,12},{5,13},{6,14},{7,15},{8,0},{9,1},... | collective-permute-start | bytes 835592 | tf_op jit(solution)/shard_map/ppermute | solution.py:74
  20.1 0.9 %collective-permute-done.4 = bf16[12,4224]{1,0:T(8,128)(2,1)S(1)} collective-permute-done((bf16[12,4224]{1,0:T(8,128)(2,1)S(1)}, bf16[12,4224]{1,0:T(8,128)(2,1)S(1)}, u32[]{:S(2)}, u32[]{:S(2)}) %collective-permute-start.4) | collective-permute-done | bytes 101408 | tf_op jit(solution)/shard_map/ppermute | solution.py:74
  21.1 1.9 %collective-permute-start.10 = (bf16[24,4224]{1,0:T(8,128)(2,1)S(1)}, bf16[24,4224]{1,0:T(8,128)(2,1)S(1)}, u32[]{:S(2)}, u32[]{:S(2)}) collective-permute-start(bf16[24,4224]{1,0:T(8,128)(2,1)S(1)} %pad_maximum_fusion.1.refs_1_), channel_id=1, source_target_pairs={{0,4},{1,3},{2,6},{3,1},{4,0},{5,7},{6,2},{7,5},{8,12},{9,11},{10,... | collective-permute-start | bytes 608264 | tf_op jit(solution)/shard_map/ppermute | solution.py:74
  23.0 0.5 %collective-permute-start.8 = (bf16[24,4224]{1,0:T(8,128)(2,1)S(1)}, bf16[24,4224]{1,0:T(8,128)(2,1)S(1)}, u32[]{:S(2)}, u32[]{:S(2)}) collective-permute-start(bf16[24,4224]{1,0:T(8,128)(2,1)S(1)} %pad_maximum_fusion.1.refs_1_), channel_id=1, source_target_pairs={{0,1},{1,0},{2,3},{3,2},{4,5},{5,4},{6,7},{7,6},{8,9},{9,8},{10,11... | collective-permute-start | bytes 608264 | tf_op jit(solution)/shard_map/ppermute | solution.py:78
  23.5 4.2 %collective-permute-done.11.refs_3_ = bf16[34,4096]{1,0:T(8,128)(2,1)S(1)} collective-permute-done((bf16[34,4096]{1,0:T(8,128)(2,1)S(1)}, bf16[34,4096]{1,0:T(8,128)(2,1)S(1)}, u32[]{:S(2)}, u32[]{:S(2)}) %collective-permute-start.11) | collective-permute-done | bytes 278560 | tf_op jit(solution)/shard_map/ppermute | solution.py:74
  27.7 1.3 %early_partials.1 = (f32[4,144]{1,0:T(4,128)S(1)}, bf16[144,4224]{1,0:T(8,128)(2,1)S(1)}) custom-call(bf16[24,4224]{1,0:T(8,128)(2,1)S(1)} %pad_maximum_fusion.refs_0_, bf16[24,4224]{1,0:T(8,128)(2,1)S(1)} %pad_maximum_fusion.1.refs_1_, bf16[24,4224]{1,0:T(8,128)(2,1)S(1)} %collective-permute-done.5.refs_2_, ...), custom_call_target="tpu_custom_call" | custom-call | tf_op jit(solution)/shard_map/early_partials/pallas_call | solution.py:265
  29.1 1.2 %late_partials.1.mine_ref = f32[4,192]{1,0:T(4,128)S(1)} custom-call(f32[4,144]{1,0:T(4,128)S(1)} %get-tuple-element.37.early_ref, bf16[144,4224]{1,0:T(8,128)(2,1)S(1)} %get-tuple-element.38.rows_ref, bf16[24,4224]{1,0:T(8,128)(2,1)S(1)} %collective-permute-done.10.mine_ref, bf16[24,4224]{1,0:T(8,128)(2,1)S(1)} %collective-permute-done.12.other_ref, ...), custom_call_target="tpu_custom_call" | custom-call | tf_op jit(solution)/shard_map/late_partials/pallas_call | solution.py:281
  30.3 0.5 %collective-permute-start.13 = (f32[4,192]{1,0:T(4,128)S(1)}, f32[4,192]{1,0:T(4,128)S(1)}, u32[]{:S(2)}, u32[]{:S(2)}) collective-permute-start(f32[4,192]{1,0:T(4,128)S(1)} %late_partials.1.mine_ref), channel_id=1, source_target_pairs={{0,1},{1,0},{2,3},{3,2},{4,5},{5,4},{6,7},{7,6},{8,9},{9,8},{10,11... | collective-permute-start | bytes 9224 | tf_op jit(solution)/shard_map/ppermute | solution.py:78
  30.8 0.8 %collective-permute-done.13.theirs_ref = f32[4,192]{1,0:T(4,128)S(1)} collective-permute-done((f32[4,192]{1,0:T(4,128)S(1)}, f32[4,192]{1,0:T(4,128)S(1)}, u32[]{:S(2)}, u32[]{:S(2)}) %collective-permute-start.13) | collective-permute-done | bytes 3104 | tf_op jit(solution)/shard_map/ppermute | solution.py:78
  31.8 1.8 %collective-permute-start.14 = (f32[4,96]{1,0:T(4,128)S(1)}, f32[4,96]{1,0:T(4,128)S(1)}, u32[]{:S(2)}, u32[]{:S(2)}) collective-permute-start(f32[4,96]{1,0:T(4,128)S(1)} %get-tuple-element.43), channel_id=1, source_target_pairs={{0,4},{1,3},{2,6},{3,1},{4,0},{5,7},{6,2},{7,5},{8,12},{9,11},{10,... | collective-permute-start | bytes 4616 | tf_op jit(solution)/shard_map/ppermute | solution.py:74
  33.6 1.9 %collective-permute-done.14.theirs_ref = f32[4,96]{1,0:T(4,128)S(1)} collective-permute-done((f32[4,96]{1,0:T(4,128)S(1)}, f32[4,96]{1,0:T(4,128)S(1)}, u32[]{:S(2)}, u32[]{:S(2)}) %collective-permute-start.14) | collective-permute-done | bytes 1568 | tf_op jit(solution)/shard_map/ppermute | solution.py:74
  35.6 1.7 %collective-permute-start.15 = (f32[4,48]{1,0:T(4,128)S(1)}, f32[4,48]{1,0:T(4,128)S(1)}, u32[]{:S(2)}, u32[]{:S(2)}) collective-permute-start(f32[4,48]{1,0:T(4,128)S(1)} %get-tuple-element.45), channel_id=1, source_target_pairs={{0,2},{1,5},{2,0},{3,7},{4,6},{5,1},{6,4},{7,3},{8,10},{9,13},{10,... | collective-permute-start | bytes 2312 | tf_op jit(solution)/shard_map/ppermute | solution.py:74
  37.3 1.9 %collective-permute-done.15.theirs_ref = f32[4,48]{1,0:T(4,128)S(1)} collective-permute-done((f32[4,48]{1,0:T(4,128)S(1)}, f32[4,48]{1,0:T(4,128)S(1)}, u32[]{:S(2)}, u32[]{:S(2)}) %collective-permute-start.15) | collective-permute-done | bytes 800 | tf_op jit(solution)/shard_map/ppermute | solution.py:74
  39.3 2.8 %collective-permute-start.16 = (f32[4,24]{1,0:T(4,128)S(1)}, f32[4,24]{1,0:T(4,128)S(1)}, u32[]{:S(2)}, u32[]{:S(2)}) collective-permute-start(f32[4,24]{1,0:T(4,128)S(1)} %get-tuple-element.47), channel_id=1, source_target_pairs={{0,16},{1,17},{2,18},{3,19},{4,20},{5,21},{6,22},{7,23},{8,24},{9,... | collective-permute-start | bytes 1160 | tf_op jit(solution)/shard_map/ppermute | solution.py:74
  42.2 1.6 %collective-permute-done.16.theirs_ref = f32[4,24]{1,0:T(4,128)S(1)} collective-permute-done((f32[4,24]{1,0:T(4,128)S(1)}, f32[4,24]{1,0:T(4,128)S(1)}, u32[]{:S(2)}, u32[]{:S(2)}) %collective-permute-start.16) | collective-permute-done | bytes 416 | tf_op jit(solution)/shard_map/ppermute | solution.py:74
  44.0 0.5 %slice_bitcast_fusion = (f32[24]{0:T(128)}, f32[24]{0:T(128)}) fusion(f32[2,24]{1,0:T(2,128)S(1)} %fusion.2), kind=kLoop, calls=%fused_computation.8 | loop fusion | bytes 384 | tf_op jit(solution)/shard_map/squeeze | solution.py:385
  (30 shorter events, 1.5 us)
Async XLA Ops:
  0.6 27.1 %copy-start = (bf16[98,4096]{1,0:T(8,128)(2,1)S(1)}, bf16[98,4096]{1,0:T(8,128)(2,1)}, u32[]{:S(2)}) copy-start(bf16[98,4096]{1,0:T(8,128)(2,1)} %refs_0_.1) | copy-start | bytes 2408452
  0.6 4.6 %collective-permute-start = (bf16[24,2048]{1,0:T(8,128)(2,1)}, bf16[24,2048]{1,0:T(8,128)(2,1)S(1)}, u32[]{:S(2)}, u32[]{:S(2)}) collective-permute-start(bf16[24,2048]{1,0:T(8,128)(2,1)} %hidden_in.1), channel_id=1, source_target_pairs={{0,1},{1,0},{2,3},{3,2},{4,5},{5,4},{6,7},{7,6},{8,9},{9,8},{10,11... | collective-permute-start | bytes 294920 | tf_op jit(solution)/shard_map/ppermute | solution.py:78
  2.5 11.4 %collective-permute-start.3 = (bf16[24,4096]{1,0:T(8,128)(2,1)S(1)}, bf16[24,4096]{1,0:T(8,128)(2,1)S(1)}, u32[]{:S(2)}, u32[]{:S(2)}) collective-permute-start(bf16[24,4096]{1,0:T(8,128)(2,1)S(1)} %get-tuple-element.29), channel_id=1, source_target_pairs={{0,8},{1,9},{2,10},{3,11},{4,12},{5,13},{6,14},{7,15},{8,0},{9,1},... | collective-permute-start | bytes 589832 | tf_op jit(solution)/shard_map/ppermute | solution.py:74
  5.4 8.4 %collective-permute-start.1 = (bf16[12,4224]{1,0:T(8,128)(2,1)S(1)}, bf16[12,4224]{1,0:T(8,128)(2,1)S(1)}, u32[]{:S(2)}, u32[]{:S(2)}) collective-permute-start(bf16[12,4224]{1,0:T(8,128)(2,1)S(1)} %normalize_rows.1), channel_id=1, source_target_pairs={{0,16},{1,17},{2,18},{3,19},{4,20},{5,21},{6,22},{7,23},{8,24},{9,... | collective-permute-start | bytes 304136 | tf_op jit(solution)/shard_map/ppermute | solution.py:74
  8.1 5.8 %collective-permute-start.2 = (bf16[12,4224]{1,0:T(8,128)(2,1)S(1)}, bf16[12,4224]{1,0:T(8,128)(2,1)S(1)}, u32[]{:S(2)}, u32[]{:S(2)}) collective-permute-start(bf16[12,4224]{1,0:T(8,128)(2,1)S(1)} %normalize_rows.1), channel_id=1, source_target_pairs={{0,2},{1,5},{2,0},{3,7},{4,6},{5,1},{6,4},{7,3},{8,10},{9,13},{10,... | collective-permute-start | bytes 304136 | tf_op jit(solution)/shard_map/ppermute | solution.py:74
  9.6 11.4 %collective-permute-start.6 = (bf16[40,4096]{1,0:T(8,128)(2,1)S(1)}, bf16[40,4096]{1,0:T(8,128)(2,1)S(1)}, u32[]{:S(2)}, u32[]{:S(2)}) collective-permute-start(bf16[40,4096]{1,0:T(8,128)(2,1)S(1)} %get-tuple-element.32), channel_id=1, source_target_pairs={{0,8},{1,9},{2,10},{3,11},{4,12},{5,13},{6,14},{7,15},{8,0},{9,1},... | collective-permute-start | bytes 983048 | tf_op jit(solution)/shard_map/ppermute | solution.py:74
  13.9 7.0 %collective-permute-start.5 = (bf16[24,4224]{1,0:T(8,128)(2,1)S(1)}, bf16[24,4224]{1,0:T(8,128)(2,1)S(1)}, u32[]{:S(2)}, u32[]{:S(2)}) collective-permute-start(bf16[24,4224]{1,0:T(8,128)(2,1)S(1)} %pad_maximum_fusion.refs_0_), channel_id=1, source_target_pairs={{0,4},{1,3},{2,6},{3,1},{4,0},{5,7},{6,2},{7,5},{8,12},{9,11},{10,... | collective-permute-start | bytes 608264 | tf_op jit(solution)/shard_map/ppermute | solution.py:74
  16.0 5.0 %collective-permute-start.4 = (bf16[12,4224]{1,0:T(8,128)(2,1)S(1)}, bf16[12,4224]{1,0:T(8,128)(2,1)S(1)}, u32[]{:S(2)}, u32[]{:S(2)}) collective-permute-start(bf16[12,4224]{1,0:T(8,128)(2,1)S(1)} %collective-permute-done.1), channel_id=1, source_target_pairs={{0,2},{1,5},{2,0},{3,7},{4,6},{5,1},{6,4},{7,3},{8,10},{9,13},{10,... | collective-permute-start | bytes 304136 | tf_op jit(solution)/shard_map/ppermute | solution.py:74
  17.5 10.2 %collective-permute-start.11 = (bf16[34,4096]{1,0:T(8,128)(2,1)S(1)}, bf16[34,4096]{1,0:T(8,128)(2,1)S(1)}, u32[]{:S(2)}, u32[]{:S(2)}) collective-permute-start(bf16[34,4096]{1,0:T(8,128)(2,1)S(1)} %get-tuple-element.39), channel_id=1, source_target_pairs={{0,8},{1,9},{2,10},{3,11},{4,12},{5,13},{6,14},{7,15},{8,0},{9,1},... | collective-permute-start | bytes 835592 | tf_op jit(solution)/shard_map/ppermute | solution.py:74
  21.1 6.6 %collective-permute-start.10 = (bf16[24,4224]{1,0:T(8,128)(2,1)S(1)}, bf16[24,4224]{1,0:T(8,128)(2,1)S(1)}, u32[]{:S(2)}, u32[]{:S(2)}) collective-permute-start(bf16[24,4224]{1,0:T(8,128)(2,1)S(1)} %pad_maximum_fusion.1.refs_1_), channel_id=1, source_target_pairs={{0,4},{1,3},{2,6},{3,1},{4,0},{5,7},{6,2},{7,5},{8,12},{9,11},{10,... | collective-permute-start | bytes 608264 | tf_op jit(solution)/shard_map/ppermute | solution.py:74
  23.0 4.7 %collective-permute-start.7 = (bf16[24,4224]{1,0:T(8,128)(2,1)S(1)}, bf16[24,4224]{1,0:T(8,128)(2,1)S(1)}, u32[]{:S(2)}, u32[]{:S(2)}) collective-permute-start(bf16[24,4224]{1,0:T(8,128)(2,1)S(1)} %pad_maximum_fusion.refs_0_), channel_id=1, source_target_pairs={{0,1},{1,0},{2,3},{3,2},{4,5},{5,4},{6,7},{7,6},{8,9},{9,8},{10,11... | collective-permute-start | bytes 608264 | tf_op jit(solution)/shard_map/ppermute | solution.py:78
  23.0 4.7 %collective-permute-start.8 = (bf16[24,4224]{1,0:T(8,128)(2,1)S(1)}, bf16[24,4224]{1,0:T(8,128)(2,1)S(1)}, u32[]{:S(2)}, u32[]{:S(2)}) collective-permute-start(bf16[24,4224]{1,0:T(8,128)(2,1)S(1)} %pad_maximum_fusion.1.refs_1_), channel_id=1, source_target_pairs={{0,1},{1,0},{2,3},{3,2},{4,5},{5,4},{6,7},{7,6},{8,9},{9,8},{10,11... | collective-permute-start | bytes 608264 | tf_op jit(solution)/shard_map/ppermute | solution.py:78
  23.5 4.2 %collective-permute-start.9 = (bf16[24,4224]{1,0:T(8,128)(2,1)S(1)}, bf16[24,4224]{1,0:T(8,128)(2,1)S(1)}, u32[]{:S(2)}, u32[]{:S(2)}) collective-permute-start(bf16[24,4224]{1,0:T(8,128)(2,1)S(1)} %collective-permute-done.5.refs_2_), channel_id=1, source_target_pairs={{0,1},{1,0},{2,3},{3,2},{4,5},{5,4},{6,7},{7,6},{8,9},{9,8},{10,11... | collective-permute-start | bytes 608264 | tf_op jit(solution)/shard_map/ppermute | solution.py:78
  27.7 1.5 %collective-permute-start.12 = (bf16[24,4224]{1,0:T(8,128)(2,1)S(1)}, bf16[24,4224]{1,0:T(8,128)(2,1)S(1)}, u32[]{:S(2)}, u32[]{:S(2)}) collective-permute-start(bf16[24,4224]{1,0:T(8,128)(2,1)S(1)} %collective-permute-done.10.mine_ref), channel_id=1, source_target_pairs={{0,1},{1,0},{2,3},{3,2},{4,5},{5,4},{6,7},{7,6},{8,9},{9,8},{10,11... | collective-permute-start | bytes 608264 | tf_op jit(solution)/shard_map/ppermute | solution.py:78
  29.1 13.0 %copy-start.1 = (s32[3]{0:T(128)S(1)}, s32[3]{0:T(128)}, u32[]{:S(2)}) copy-start(s32[3]{0:T(128)} %param.13) | copy-start | bytes 40
  29.1 13.0 %copy-start.2 = (s32[3]{0:T(128)S(1)}, s32[3]{0:T(128)}, u32[]{:S(2)}) copy-start(s32[3]{0:T(128)} %param.12) | copy-start | bytes 40
  30.3 1.3 %collective-permute-start.13 = (f32[4,192]{1,0:T(4,128)S(1)}, f32[4,192]{1,0:T(4,128)S(1)}, u32[]{:S(2)}, u32[]{:S(2)}) collective-permute-start(f32[4,192]{1,0:T(4,128)S(1)} %late_partials.1.mine_ref), channel_id=1, source_target_pairs={{0,1},{1,0},{2,3},{3,2},{4,5},{5,4},{6,7},{7,6},{8,9},{9,8},{10,11... | collective-permute-start | bytes 9224 | tf_op jit(solution)/shard_map/ppermute | solution.py:78
  31.8 3.7 %collective-permute-start.14 = (f32[4,96]{1,0:T(4,128)S(1)}, f32[4,96]{1,0:T(4,128)S(1)}, u32[]{:S(2)}, u32[]{:S(2)}) collective-permute-start(f32[4,96]{1,0:T(4,128)S(1)} %get-tuple-element.43), channel_id=1, source_target_pairs={{0,4},{1,3},{2,6},{3,1},{4,0},{5,7},{6,2},{7,5},{8,12},{9,11},{10,... | collective-permute-start | bytes 4616 | tf_op jit(solution)/shard_map/ppermute | solution.py:74
  35.6 3.7 %collective-permute-start.15 = (f32[4,48]{1,0:T(4,128)S(1)}, f32[4,48]{1,0:T(4,128)S(1)}, u32[]{:S(2)}, u32[]{:S(2)}) collective-permute-start(f32[4,48]{1,0:T(4,128)S(1)} %get-tuple-element.45), channel_id=1, source_target_pairs={{0,2},{1,5},{2,0},{3,7},{4,6},{5,1},{6,4},{7,3},{8,10},{9,13},{10,... | collective-permute-start | bytes 2312 | tf_op jit(solution)/shard_map/ppermute | solution.py:74
  39.3 4.5 %collective-permute-start.16 = (f32[4,24]{1,0:T(4,128)S(1)}, f32[4,24]{1,0:T(4,128)S(1)}, u32[]{:S(2)}, u32[]{:S(2)}) collective-permute-start(f32[4,24]{1,0:T(4,128)S(1)} %get-tuple-element.47), channel_id=1, source_target_pairs={{0,16},{1,17},{2,18},{3,19},{4,20},{5,21},{6,22},{7,23},{8,24},{9,... | collective-permute-start | bytes 1160 | tf_op jit(solution)/shard_map/ppermute | solution.py:74

commit v4 on v3

--- a/solution.py
+++ b/solution.py
@@ -303,12 +303,16 @@
             out[pl.ds(k, 1), :] = blocks_of(value, group, order)
 
 
-def finish_kernel(mine_ref, theirs_ref, out_ref):
+def finish_kernel(mine_ref, theirs_ref, live_ref, logprob_ref, entropy_ref):
     mine, theirs = ([ref[pl.ds(k, 1), :] for k in range(4)] for ref in (mine_ref, theirs_ref))
     row_top, row_total, row_spread, target_hit = merge(mine, theirs)
     log_total = jnp.log(row_total)
-    out_ref[pl.ds(0, 1), :] = target_hit - row_top - log_total
-    out_ref[pl.ds(1, 1), :] = log_total - row_spread / row_total
+    half = mine_ref.shape[1] // 2
+    results = (target_hit - row_top - log_total, log_total - row_spread / row_total)
+    for value, out in zip(results, (logprob_ref, entropy_ref)):
+        turned = blocks_of(value, half, (1, 0))
+        value = jnp.where(lax.axis_index("tp") == 0, value, turned)
+        out[...] = jnp.where(live_ref[...] > 0, value, 0.0)
 
 
 def merge_and_split(mine, theirs, group, orders, theirs_order=()):
@@ -323,23 +327,22 @@
     )(in_vmem(mine), in_vmem(theirs))
 
 
-def finish(mine, theirs):
+def finish(mine, theirs, live):
     vmem = pl.BlockSpec(memory_space=pltpu.VMEM)
     return pl.pallas_call(
         finish_kernel,
-        out_shape=pltpu.VMEM((2, mine.shape[1]), jnp.float32),
-        in_specs=[vmem] * 2,
-        out_specs=vmem,
+        out_shape=[jax.ShapeDtypeStruct((1, mine.shape[1]), jnp.float32)] * 2,
+        in_specs=[vmem] * 3,
+        out_specs=[vmem] * 2,
         compiler_params=pltpu.CompilerParams(vmem_limit_bytes=KERNEL_VMEM),
         name="finish",
-    )(in_vmem(mine), in_vmem(theirs))
+    )(in_vmem(mine), in_vmem(theirs), in_vmem(live))
 
 
 def paired(hidden, norm_gain, norm_bias, unembed, targets, span_start, span_end):
     slot_count = hidden.shape[0]
     half = slot_count // 2
     vocab_part = unembed.shape[0]
-    first_core = lax.axis_index("tp") == 0
 
     cuts = [0, *[sum(CHUNKS[: k + 1]) for k in range(len(CHUNKS))], vocab_part]
     other = core_swap(hidden)
@@ -376,13 +379,9 @@
         keep, exchange(give, SECOND), half, ((0, 2, 4, 5), (1, 3, 6, 7))
     )
     keep, give = merge_and_split(keep, exchange(give, FIRST), half, ((0, 2), (1, 3)))
-    result = finish(keep, exchange(give, FAR))
-    both = jnp.where(
-        first_core, result, jnp.concatenate([result[:, half:], result[:, :half]], axis=1)
-    )
-    live = live_mask(span_start, span_end, slot_count)
-    both = jnp.where(live, both, 0.0)
-    return both[0], both[1]
+    live = live_mask(span_start, span_end, slot_count).astype(jnp.int32).reshape(1, -1)
+    logprob, entropy = finish(keep, exchange(give, FAR), live)
+    return logprob.reshape(-1), entropy.reshape(-1)
 
 
 def solution(mesh):

time: 44.7 us -> 44.6 us (level)
  local copies, waits for them, and re-layouts: 0.61 us -> 0.01 us
  Pallas kernels: 4.4 us -> 5 us
    pallas_call x1, Pallas kernels: 0.01 us -> 0.61 us  [finish(): pl.pallas_call(finish_kernel, out_shape=[jax.ShapeDtypeStruct((1, mine.sh...]
    squeeze x1 -> x0, local copies, waits for them, and re-layouts: 0.53 us -> none  [paired(): return (both[0], both[1])]
where the time goes in v4:
time: 44.6 us; the launch traced here: 44.5 us
  starting transfers between devices  23.2 us (52%)
  waiting for transfers between devices  15.3 us (34%)
  Pallas kernels  5 us (11%)
  between operations  0.74 us (2%)
    ppermute x11, starting transfers between devices, exchange(): return lax.ppermute(value, ('req', 'tp'), pairs)  21.6 us
    ppermute x11, waiting for transfers between devices, exchange(): return lax.ppermute(value, ('req', 'tp'), pairs)  14.4 us
    ppermute x6, starting transfers between devices, core_swap(): return lax.ppermute(value, 'tp', [(0, 1), (1, 0)])  1.59 us
    pallas_call x1, Pallas kernels, early_partials(): pl.pallas_call(functools.partial(early_kernel, places, vocab_part, len(pi...  1.34 us
    pallas_call x1, Pallas kernels, stage(): pl.pallas_call(functools.partial(stage_kernel, cuts, half), out_shape=[pl...  1.33 us
    pallas_call x1, Pallas kernels, late_partials(): pl.pallas_call(functools.partial(late_kernel, places, vocab_part), out_sh...  1.19 us
    ppermute x6, waiting for transfers between devices, core_swap(): return lax.ppermute(value, 'tp', [(0, 1), (1, 0)])  0.9 us
  transfers between devices with their start and end apart: 17, of which 8 were waited for; matrix products, arithmetic and copies ran while one was open for 0% of the time, Pallas kernels for 6%

profile of v4, /device:TPU:0, one launch (start us, length us, event | category | flops | bytes accessed | tf_op | source)
XLA Modules:
  0.0 44.5 jit_solution(10410097712085691348)
XLA Ops:
  0.6 0.6 %collective-permute-start = (bf16[24,2048]{1,0:T(8,128)(2,1)}, bf16[24,2048]{1,0:T(8,128)(2,1)S(1)}, u32[]{:S(2)}, u32[]{:S(2)}) collective-permute-start(bf16[24,2048]{1,0:T(8,128)(2,1)} %hidden_in.1), channel_id=1, source_target_pairs={{0,1},{1,0},{2,3},{3,2},{4,5},{5,4},{6,7},{7,6},{8,9},{9,8},{10,11... | collective-permute-start | bytes 294920 | tf_op jit(solution)/shard_map/ppermute | solution.py:78
  1.2 1.3 %stage.1 = (bf16[24,2048]{1,0:T(8,128)(2,1)S(1)}, f32[1,4096]{1,0:T(1,128)S(1)}, f32[1,4096]{1,0:T(1,128)S(1)}, bf16[12,128]{1,0:T(8,128)(2,1)S(1)}, bf16[24,409...) custom-call(bf16[24,2048]{1,0:T(8,128)(2,1)} %hidden_in.1, f32[1,4096]{1,0:T(1,128)} %bitcast.7, ...), custom_call_target="tpu_custom_call" | custom-call | tf_op jit(solution)/shard_map/stage/pallas_call | solution.py:124
  2.5 2.7 %collective-permute-start.3 = (bf16[24,4096]{1,0:T(8,128)(2,1)S(1)}, bf16[24,4096]{1,0:T(8,128)(2,1)S(1)}, u32[]{:S(2)}, u32[]{:S(2)}) collective-permute-start(bf16[24,4096]{1,0:T(8,128)(2,1)S(1)} %get-tuple-element.31), channel_id=1, source_target_pairs={{0,8},{1,9},{2,10},{3,11},{4,12},{5,13},{6,14},{7,15},{8,0},{9,1},... | collective-permute-start | bytes 589832 | tf_op jit(solution)/shard_map/ppermute | solution.py:74
  5.4 2.7 %collective-permute-start.1 = (bf16[12,4224]{1,0:T(8,128)(2,1)S(1)}, bf16[12,4224]{1,0:T(8,128)(2,1)S(1)}, u32[]{:S(2)}, u32[]{:S(2)}) collective-permute-start(bf16[12,4224]{1,0:T(8,128)(2,1)S(1)} %normalize_rows.1), channel_id=1, source_target_pairs={{0,16},{1,17},{2,18},{3,19},{4,20},{5,21},{6,22},{7,23},{8,24},{9,... | collective-permute-start | bytes 304136 | tf_op jit(solution)/shard_map/ppermute | solution.py:74
  8.1 1.5 %collective-permute-start.2 = (bf16[12,4224]{1,0:T(8,128)(2,1)S(1)}, bf16[12,4224]{1,0:T(8,128)(2,1)S(1)}, u32[]{:S(2)}, u32[]{:S(2)}) collective-permute-start(bf16[12,4224]{1,0:T(8,128)(2,1)S(1)} %normalize_rows.1), channel_id=1, source_target_pairs={{0,2},{1,5},{2,0},{3,7},{4,6},{5,1},{6,4},{7,3},{8,10},{9,13},{10,... | collective-permute-start | bytes 304136 | tf_op jit(solution)/shard_map/ppermute | solution.py:74
  10.0 3.8 %collective-permute-done.3.refs_7_.refs_1_ = bf16[24,4096]{1,0:T(8,128)(2,1)S(1)} collective-permute-done((bf16[24,4096]{1,0:T(8,128)(2,1)S(1)}, bf16[24,4096]{1,0:T(8,128)(2,1)S(1)}, u32[]{:S(2)}, u32[]{:S(2)}) %collective-permute-start.3) | collective-permute-done | bytes 196640 | tf_op jit(solution)/shard_map/ppermute | solution.py:74
  13.9 2.0 %collective-permute-start.5 = (bf16[24,4224]{1,0:T(8,128)(2,1)S(1)}, bf16[24,4224]{1,0:T(8,128)(2,1)S(1)}, u32[]{:S(2)}, u32[]{:S(2)}) collective-permute-start(bf16[24,4224]{1,0:T(8,128)(2,1)S(1)} %pad_maximum_fusion.refs_0_), channel_id=1, source_target_pairs={{0,4},{1,3},{2,6},{3,1},{4,0},{5,7},{6,2},{7,5},{8,12},{9,11},{10,... | collective-permute-start | bytes 608264 | tf_op jit(solution)/shard_map/ppermute | solution.py:74
  16.0 1.5 %collective-permute-start.4 = (bf16[12,4224]{1,0:T(8,128)(2,1)S(1)}, bf16[12,4224]{1,0:T(8,128)(2,1)S(1)}, u32[]{:S(2)}, u32[]{:S(2)}) collective-permute-start(bf16[12,4224]{1,0:T(8,128)(2,1)S(1)} %collective-permute-done.1), channel_id=1, source_target_pairs={{0,2},{1,5},{2,0},{3,7},{4,6},{5,1},{6,4},{7,3},{8,10},{9,13},{10,... | collective-permute-start | bytes 304136 | tf_op jit(solution)/shard_map/ppermute | solution.py:74
  17.5 2.6 %collective-permute-start.11 = (bf16[34,4096]{1,0:T(8,128)(2,1)S(1)}, bf16[34,4096]{1,0:T(8,128)(2,1)S(1)}, u32[]{:S(2)}, u32[]{:S(2)}) collective-permute-start(bf16[34,4096]{1,0:T(8,128)(2,1)S(1)} %get-tuple-element.41), channel_id=1, source_target_pairs={{0,8},{1,9},{2,10},{3,11},{4,12},{5,13},{6,14},{7,15},{8,0},{9,1},... | collective-permute-start | bytes 835592 | tf_op jit(solution)/shard_map/ppermute | solution.py:74
  20.1 0.9 %collective-permute-done.4 = bf16[12,4224]{1,0:T(8,128)(2,1)S(1)} collective-permute-done((bf16[12,4224]{1,0:T(8,128)(2,1)S(1)}, bf16[12,4224]{1,0:T(8,128)(2,1)S(1)}, u32[]{:S(2)}, u32[]{:S(2)}) %collective-permute-start.4) | collective-permute-done | bytes 101408 | tf_op jit(solution)/shard_map/ppermute | solution.py:74
  21.1 1.9 %collective-permute-start.10 = (bf16[24,4224]{1,0:T(8,128)(2,1)S(1)}, bf16[24,4224]{1,0:T(8,128)(2,1)S(1)}, u32[]{:S(2)}, u32[]{:S(2)}) collective-permute-start(bf16[24,4224]{1,0:T(8,128)(2,1)S(1)} %pad_maximum_fusion.1.refs_1_), channel_id=1, source_target_pairs={{0,4},{1,3},{2,6},{3,1},{4,0},{5,7},{6,2},{7,5},{8,12},{9,11},{10,... | collective-permute-start | bytes 608264 | tf_op jit(solution)/shard_map/ppermute | solution.py:74
  23.0 0.5 %collective-permute-start.8 = (bf16[24,4224]{1,0:T(8,128)(2,1)S(1)}, bf16[24,4224]{1,0:T(8,128)(2,1)S(1)}, u32[]{:S(2)}, u32[]{:S(2)}) collective-permute-start(bf16[24,4224]{1,0:T(8,128)(2,1)S(1)} %pad_maximum_fusion.1.refs_1_), channel_id=1, source_target_pairs={{0,1},{1,0},{2,3},{3,2},{4,5},{5,4},{6,7},{7,6},{8,9},{9,8},{10,11... | collective-permute-start | bytes 608264 | tf_op jit(solution)/shard_map/ppermute | solution.py:78
  23.5 4.2 %collective-permute-done.11.refs_3_ = bf16[34,4096]{1,0:T(8,128)(2,1)S(1)} collective-permute-done((bf16[34,4096]{1,0:T(8,128)(2,1)S(1)}, bf16[34,4096]{1,0:T(8,128)(2,1)S(1)}, u32[]{:S(2)}, u32[]{:S(2)}) %collective-permute-start.11) | collective-permute-done | bytes 278560 | tf_op jit(solution)/shard_map/ppermute | solution.py:74
  27.7 1.3 %early_partials.1 = (f32[4,144]{1,0:T(4,128)S(1)}, bf16[144,4224]{1,0:T(8,128)(2,1)S(1)}) custom-call(bf16[24,4224]{1,0:T(8,128)(2,1)S(1)} %pad_maximum_fusion.refs_0_, bf16[24,4224]{1,0:T(8,128)(2,1)S(1)} %pad_maximum_fusion.1.refs_1_, bf16[24,4224]{1,0:T(8,128)(2,1)S(1)} %collective-permute-done.5.refs_2_, ...), custom_call_target="tpu_custom_call" | custom-call | tf_op jit(solution)/shard_map/early_partials/pallas_call | solution.py:265
  29.1 1.2 %late_partials.1.mine_ref = f32[4,192]{1,0:T(4,128)S(1)} custom-call(f32[4,144]{1,0:T(4,128)S(1)} %get-tuple-element.39.early_ref, bf16[144,4224]{1,0:T(8,128)(2,1)S(1)} %get-tuple-element.40.rows_ref, bf16[24,4224]{1,0:T(8,128)(2,1)S(1)} %collective-permute-done.10.mine_ref, bf16[24,4224]{1,0:T(8,128)(2,1)S(1)} %collective-permute-done.12.other_ref, ...), custom_call_target="tpu_custom_call" | custom-call | tf_op jit(solution)/shard_map/late_partials/pallas_call | solution.py:281
  30.3 0.5 %collective-permute-start.13 = (f32[4,192]{1,0:T(4,128)S(1)}, f32[4,192]{1,0:T(4,128)S(1)}, u32[]{:S(2)}, u32[]{:S(2)}) collective-permute-start(f32[4,192]{1,0:T(4,128)S(1)} %late_partials.1.mine_ref), channel_id=1, source_target_pairs={{0,1},{1,0},{2,3},{3,2},{4,5},{5,4},{6,7},{7,6},{8,9},{9,8},{10,11... | collective-permute-start | bytes 9224 | tf_op jit(solution)/shard_map/ppermute | solution.py:78
  30.8 0.8 %collective-permute-done.13.theirs_ref = f32[4,192]{1,0:T(4,128)S(1)} collective-permute-done((f32[4,192]{1,0:T(4,128)S(1)}, f32[4,192]{1,0:T(4,128)S(1)}, u32[]{:S(2)}, u32[]{:S(2)}) %collective-permute-start.13) | collective-permute-done | bytes 3104 | tf_op jit(solution)/shard_map/ppermute | solution.py:78
  31.8 1.8 %collective-permute-start.14 = (f32[4,96]{1,0:T(4,128)S(1)}, f32[4,96]{1,0:T(4,128)S(1)}, u32[]{:S(2)}, u32[]{:S(2)}) collective-permute-start(f32[4,96]{1,0:T(4,128)S(1)} %get-tuple-element.45), channel_id=1, source_target_pairs={{0,4},{1,3},{2,6},{3,1},{4,0},{5,7},{6,2},{7,5},{8,12},{9,11},{10,... | collective-permute-start | bytes 4616 | tf_op jit(solution)/shard_map/ppermute | solution.py:74
  33.6 1.9 %collective-permute-done.14.theirs_ref = f32[4,96]{1,0:T(4,128)S(1)} collective-permute-done((f32[4,96]{1,0:T(4,128)S(1)}, f32[4,96]{1,0:T(4,128)S(1)}, u32[]{:S(2)}, u32[]{:S(2)}) %collective-permute-start.14) | collective-permute-done | bytes 1568 | tf_op jit(solution)/shard_map/ppermute | solution.py:74
  35.6 1.7 %collective-permute-start.15 = (f32[4,48]{1,0:T(4,128)S(1)}, f32[4,48]{1,0:T(4,128)S(1)}, u32[]{:S(2)}, u32[]{:S(2)}) collective-permute-start(f32[4,48]{1,0:T(4,128)S(1)} %get-tuple-element.47), channel_id=1, source_target_pairs={{0,2},{1,5},{2,0},{3,7},{4,6},{5,1},{6,4},{7,3},{8,10},{9,13},{10,... | collective-permute-start | bytes 2312 | tf_op jit(solution)/shard_map/ppermute | solution.py:74
  37.4 1.8 %collective-permute-done.15.theirs_ref = f32[4,48]{1,0:T(4,128)S(1)} collective-permute-done((f32[4,48]{1,0:T(4,128)S(1)}, f32[4,48]{1,0:T(4,128)S(1)}, u32[]{:S(2)}, u32[]{:S(2)}) %collective-permute-start.15) | collective-permute-done | bytes 800 | tf_op jit(solution)/shard_map/ppermute | solution.py:74
  39.3 2.8 %collective-permute-start.16 = (f32[4,24]{1,0:T(4,128)S(1)}, f32[4,24]{1,0:T(4,128)S(1)}, u32[]{:S(2)}, u32[]{:S(2)}) collective-permute-start(f32[4,24]{1,0:T(4,128)S(1)} %get-tuple-element.49), channel_id=1, source_target_pairs={{0,16},{1,17},{2,18},{3,19},{4,20},{5,21},{6,22},{7,23},{8,24},{9,... | collective-permute-start | bytes 1160 | tf_op jit(solution)/shard_map/ppermute | solution.py:74
  42.1 1.7 %collective-permute-done.16.theirs_ref = f32[4,24]{1,0:T(4,128)S(1)} collective-permute-done((f32[4,24]{1,0:T(4,128)S(1)}, f32[4,24]{1,0:T(4,128)S(1)}, u32[]{:S(2)}, u32[]{:S(2)}) %collective-permute-start.16) | collective-permute-done | bytes 416 | tf_op jit(solution)/shard_map/ppermute | solution.py:74
  43.9 0.6 %finish.1 = (f32[1,24]{1,0:T(1,128)}, f32[1,24]{1,0:T(1,128)}) custom-call(f32[4,24]{1,0:T(4,128)S(1)} %get-tuple-element.48.mine_ref, f32[4,24]{1,0:T(4,128)S(1)} %collective-permute-done.16.theirs_ref, s32[1,24]{1,0:T(1,128)S(1)} %convert_bitcast_fusion.live_ref), custom_call_target="tpu_custom_call" | custom-call | tf_op jit(solution)/shard_map/finish/pallas_call | solution.py:332
  (28 shorter events, 1.3 us)
Async XLA Ops:
  0.6 27.1 %copy-start = (bf16[98,4096]{1,0:T(8,128)(2,1)S(1)}, bf16[98,4096]{1,0:T(8,128)(2,1)}, u32[]{:S(2)}) copy-start(bf16[98,4096]{1,0:T(8,128)(2,1)} %refs_0_.1) | copy-start | bytes 2408452
  0.6 4.6 %collective-permute-start = (bf16[24,2048]{1,0:T(8,128)(2,1)}, bf16[24,2048]{1,0:T(8,128)(2,1)S(1)}, u32[]{:S(2)}, u32[]{:S(2)}) collective-permute-start(bf16[24,2048]{1,0:T(8,128)(2,1)} %hidden_in.1), channel_id=1, source_target_pairs={{0,1},{1,0},{2,3},{3,2},{4,5},{5,4},{6,7},{7,6},{8,9},{9,8},{10,11... | collective-permute-start | bytes 294920 | tf_op jit(solution)/shard_map/ppermute | solution.py:78
  2.5 11.4 %collective-permute-start.3 = (bf16[24,4096]{1,0:T(8,128)(2,1)S(1)}, bf16[24,4096]{1,0:T(8,128)(2,1)S(1)}, u32[]{:S(2)}, u32[]{:S(2)}) collective-permute-start(bf16[24,4096]{1,0:T(8,128)(2,1)S(1)} %get-tuple-element.31), channel_id=1, source_target_pairs={{0,8},{1,9},{2,10},{3,11},{4,12},{5,13},{6,14},{7,15},{8,0},{9,1},... | collective-permute-start | bytes 589832 | tf_op jit(solution)/shard_map/ppermute | solution.py:74
  5.4 8.4 %collective-permute-start.1 = (bf16[12,4224]{1,0:T(8,128)(2,1)S(1)}, bf16[12,4224]{1,0:T(8,128)(2,1)S(1)}, u32[]{:S(2)}, u32[]{:S(2)}) collective-permute-start(bf16[12,4224]{1,0:T(8,128)(2,1)S(1)} %normalize_rows.1), channel_id=1, source_target_pairs={{0,16},{1,17},{2,18},{3,19},{4,20},{5,21},{6,22},{7,23},{8,24},{9,... | collective-permute-start | bytes 304136 | tf_op jit(solution)/shard_map/ppermute | solution.py:74
  8.1 5.8 %collective-permute-start.2 = (bf16[12,4224]{1,0:T(8,128)(2,1)S(1)}, bf16[12,4224]{1,0:T(8,128)(2,1)S(1)}, u32[]{:S(2)}, u32[]{:S(2)}) collective-permute-start(bf16[12,4224]{1,0:T(8,128)(2,1)S(1)} %normalize_rows.1), channel_id=1, source_target_pairs={{0,2},{1,5},{2,0},{3,7},{4,6},{5,1},{6,4},{7,3},{8,10},{9,13},{10,... | collective-permute-start | bytes 304136 | tf_op jit(solution)/shard_map/ppermute | solution.py:74
  9.6 11.4 %collective-permute-start.6 = (bf16[40,4096]{1,0:T(8,128)(2,1)S(1)}, bf16[40,4096]{1,0:T(8,128)(2,1)S(1)}, u32[]{:S(2)}, u32[]{:S(2)}) collective-permute-start(bf16[40,4096]{1,0:T(8,128)(2,1)S(1)} %get-tuple-element.34), channel_id=1, source_target_pairs={{0,8},{1,9},{2,10},{3,11},{4,12},{5,13},{6,14},{7,15},{8,0},{9,1},... | collective-permute-start | bytes 983048 | tf_op jit(solution)/shard_map/ppermute | solution.py:74
  13.9 7.0 %collective-permute-start.5 = (bf16[24,4224]{1,0:T(8,128)(2,1)S(1)}, bf16[24,4224]{1,0:T(8,128)(2,1)S(1)}, u32[]{:S(2)}, u32[]{:S(2)}) collective-permute-start(bf16[24,4224]{1,0:T(8,128)(2,1)S(1)} %pad_maximum_fusion.refs_0_), channel_id=1, source_target_pairs={{0,4},{1,3},{2,6},{3,1},{4,0},{5,7},{6,2},{7,5},{8,12},{9,11},{10,... | collective-permute-start | bytes 608264 | tf_op jit(solution)/shard_map/ppermute | solution.py:74
  16.0 5.0 %collective-permute-start.4 = (bf16[12,4224]{1,0:T(8,128)(2,1)S(1)}, bf16[12,4224]{1,0:T(8,128)(2,1)S(1)}, u32[]{:S(2)}, u32[]{:S(2)}) collective-permute-start(bf16[12,4224]{1,0:T(8,128)(2,1)S(1)} %collective-permute-done.1), channel_id=1, source_target_pairs={{0,2},{1,5},{2,0},{3,7},{4,6},{5,1},{6,4},{7,3},{8,10},{9,13},{10,... | collective-permute-start | bytes 304136 | tf_op jit(solution)/shard_map/ppermute | solution.py:74
  17.5 10.2 %collective-permute-start.11 = (bf16[34,4096]{1,0:T(8,128)(2,1)S(1)}, bf16[34,4096]{1,0:T(8,128)(2,1)S(1)}, u32[]{:S(2)}, u32[]{:S(2)}) collective-permute-start(bf16[34,4096]{1,0:T(8,128)(2,1)S(1)} %get-tuple-element.41), channel_id=1, source_target_pairs={{0,8},{1,9},{2,10},{3,11},{4,12},{5,13},{6,14},{7,15},{8,0},{9,1},... | collective-permute-start | bytes 835592 | tf_op jit(solution)/shard_map/ppermute | solution.py:74
  21.1 6.6 %collective-permute-start.10 = (bf16[24,4224]{1,0:T(8,128)(2,1)S(1)}, bf16[24,4224]{1,0:T(8,128)(2,1)S(1)}, u32[]{:S(2)}, u32[]{:S(2)}) collective-permute-start(bf16[24,4224]{1,0:T(8,128)(2,1)S(1)} %pad_maximum_fusion.1.refs_1_), channel_id=1, source_target_pairs={{0,4},{1,3},{2,6},{3,1},{4,0},{5,7},{6,2},{7,5},{8,12},{9,11},{10,... | collective-permute-start | bytes 608264 | tf_op jit(solution)/shard_map/ppermute | solution.py:74
  23.0 4.7 %collective-permute-start.7 = (bf16[24,4224]{1,0:T(8,128)(2,1)S(1)}, bf16[24,4224]{1,0:T(8,128)(2,1)S(1)}, u32[]{:S(2)}, u32[]{:S(2)}) collective-permute-start(bf16[24,4224]{1,0:T(8,128)(2,1)S(1)} %pad_maximum_fusion.refs_0_), channel_id=1, source_target_pairs={{0,1},{1,0},{2,3},{3,2},{4,5},{5,4},{6,7},{7,6},{8,9},{9,8},{10,11... | collective-permute-start | bytes 608264 | tf_op jit(solution)/shard_map/ppermute | solution.py:78
  23.0 4.7 %collective-permute-start.8 = (bf16[24,4224]{1,0:T(8,128)(2,1)S(1)}, bf16[24,4224]{1,0:T(8,128)(2,1)S(1)}, u32[]{:S(2)}, u32[]{:S(2)}) collective-permute-start(bf16[24,4224]{1,0:T(8,128)(2,1)S(1)} %pad_maximum_fusion.1.refs_1_), channel_id=1, source_target_pairs={{0,1},{1,0},{2,3},{3,2},{4,5},{5,4},{6,7},{7,6},{8,9},{9,8},{10,11... | collective-permute-start | bytes 608264 | tf_op jit(solution)/shard_map/ppermute | solution.py:78
  23.5 4.2 %collective-permute-start.9 = (bf16[24,4224]{1,0:T(8,128)(2,1)S(1)}, bf16[24,4224]{1,0:T(8,128)(2,1)S(1)}, u32[]{:S(2)}, u32[]{:S(2)}) collective-permute-start(bf16[24,4224]{1,0:T(8,128)(2,1)S(1)} %collective-permute-done.5.refs_2_), channel_id=1, source_target_pairs={{0,1},{1,0},{2,3},{3,2},{4,5},{5,4},{6,7},{7,6},{8,9},{9,8},{10,11... | collective-permute-start | bytes 608264 | tf_op jit(solution)/shard_map/ppermute | solution.py:78
  27.7 1.5 %collective-permute-start.12 = (bf16[24,4224]{1,0:T(8,128)(2,1)S(1)}, bf16[24,4224]{1,0:T(8,128)(2,1)S(1)}, u32[]{:S(2)}, u32[]{:S(2)}) collective-permute-start(bf16[24,4224]{1,0:T(8,128)(2,1)S(1)} %collective-permute-done.10.mine_ref), channel_id=1, source_target_pairs={{0,1},{1,0},{2,3},{3,2},{4,5},{5,4},{6,7},{7,6},{8,9},{9,8},{10,11... | collective-permute-start | bytes 608264 | tf_op jit(solution)/shard_map/ppermute | solution.py:78
  29.1 8.2 %copy-start.1 = (s32[3]{0:T(128)S(1)}, s32[3]{0:T(128)}, u32[]{:S(2)}) copy-start(s32[3]{0:T(128)} %param.13) | copy-start | bytes 40
  29.1 8.2 %copy-start.2 = (s32[3]{0:T(128)S(1)}, s32[3]{0:T(128)}, u32[]{:S(2)}) copy-start(s32[3]{0:T(128)} %param.12) | copy-start | bytes 40
  30.3 1.3 %collective-permute-start.13 = (f32[4,192]{1,0:T(4,128)S(1)}, f32[4,192]{1,0:T(4,128)S(1)}, u32[]{:S(2)}, u32[]{:S(2)}) collective-permute-start(f32[4,192]{1,0:T(4,128)S(1)} %late_partials.1.mine_ref), channel_id=1, source_target_pairs={{0,1},{1,0},{2,3},{3,2},{4,5},{5,4},{6,7},{7,6},{8,9},{9,8},{10,11... | collective-permute-start | bytes 9224 | tf_op jit(solution)/shard_map/ppermute | solution.py:78
  31.8 3.7 %collective-permute-start.14 = (f32[4,96]{1,0:T(4,128)S(1)}, f32[4,96]{1,0:T(4,128)S(1)}, u32[]{:S(2)}, u32[]{:S(2)}) collective-permute-start(f32[4,96]{1,0:T(4,128)S(1)} %get-tuple-element.45), channel_id=1, source_target_pairs={{0,4},{1,3},{2,6},{3,1},{4,0},{5,7},{6,2},{7,5},{8,12},{9,11},{10,... | collective-permute-start | bytes 4616 | tf_op jit(solution)/shard_map/ppermute | solution.py:74
  35.6 3.7 %collective-permute-start.15 = (f32[4,48]{1,0:T(4,128)S(1)}, f32[4,48]{1,0:T(4,128)S(1)}, u32[]{:S(2)}, u32[]{:S(2)}) collective-permute-start(f32[4,48]{1,0:T(4,128)S(1)} %get-tuple-element.47), channel_id=1, source_target_pairs={{0,2},{1,5},{2,0},{3,7},{4,6},{5,1},{6,4},{7,3},{8,10},{9,13},{10,... | collective-permute-start | bytes 2312 | tf_op jit(solution)/shard_map/ppermute | solution.py:74
  39.3 4.5 %collective-permute-start.16 = (f32[4,24]{1,0:T(4,128)S(1)}, f32[4,24]{1,0:T(4,128)S(1)}, u32[]{:S(2)}, u32[]{:S(2)}) collective-permute-start(f32[4,24]{1,0:T(4,128)S(1)} %get-tuple-element.49), channel_id=1, source_target_pairs={{0,16},{1,17},{2,18},{3,19},{4,20},{5,21},{6,22},{7,23},{8,24},{9,... | collective-permute-start | bytes 1160 | tf_op jit(solution)/shard_map/ppermute | solution.py:74
